TPU v7x, 32 devices: a whole 2x2x4 slice. The times are simulated.
32 devices in a mesh: dp: 8 (over z, x), tensor: 4 (over y, core).
Axes of the slice: x: 2, y: 2, z: 4, core: 2. Of those that a mesh axis runs over, the one named last changes fastest.
Arguments:
- tokens: bfloat16 [32768, 768], P(('dp', 'tensor')), may hold values from -6 to 6
- query_weight: bfloat16 [768, 768], P('dp', 'tensor'), may hold values from -0.21875 to 0.21875
- key_weight: bfloat16 [768, 768], P('dp', 'tensor'), may hold values from -0.21875 to 0.21875
- value_weight: bfloat16 [768, 768], P('dp', 'tensor'), may hold values from -0.21875 to 0.21875
- output_weight: bfloat16 [768, 768], P('tensor', 'dp'), may hold values from -3.5 to 3.5
- query_bias: bfloat16 [12, 64], P('tensor', 'dp'), may hold values from -3 to 3
- value_bias: bfloat16 [12, 64], P('tensor', 'dp'), may hold values from -0.109375 to 0.109375
- output_bias: float32 [768], P(('dp', 'tensor')), may hold values from -1.75 to 1.75
- first_gain: float32 [768], P(('dp', 'tensor')), may hold values from 0.5 to 1.5
- first_shift: float32 [768], P(('dp', 'tensor')), may hold values from -1.75 to 1.75
- up_weight: bfloat16 [768, 3072], P('dp', 'tensor'), may hold values from -0.21875 to 0.21875
- up_bias: bfloat16 [48, 64], P('tensor', 'dp'), may hold values from -3 to 3
- down_weight: bfloat16 [3072, 768], P('tensor', 'dp'), may hold values from -0.109375 to 0.109375
- down_bias: float32 [768], P(('dp', 'tensor')), may hold values from -1.75 to 1.75
- second_gain: float32 [768], P(('dp', 'tensor')), may hold values from 0.5 to 1.5
- second_shift: float32 [768], P(('dp', 'tensor')), may hold values from -1.75 to 1.75
- cotangent: bfloat16 [32768, 768], P(('dp', 'tensor')), may hold values from -6 to 6
Outputs:
- layer_output: bfloat16 [32768, 768], P(('dp', 'tensor'))
- grad_tokens: float32 [32768, 768], P(('dp', 'tensor'))
- grad_query_weight: float32 [768, 768], P('dp', 'tensor')
- grad_key_weight: float32 [768, 768], P('dp', 'tensor')
- grad_value_weight: float32 [768, 768], P('dp', 'tensor')
- grad_output_weight: float32 [768, 768], P('tensor', 'dp')
- grad_query_bias: float32 [12, 64], P('tensor', 'dp')
- grad_value_bias: float32 [12, 64], P('tensor', 'dp')
- grad_output_bias: float32 [768], P(('dp', 'tensor'))
- grad_first_gain: float32 [768], P(('dp', 'tensor'))
- grad_first_shift: float32 [768], P(('dp', 'tensor'))
- grad_up_weight: float32 [768, 3072], P('dp', 'tensor')
- grad_up_bias: float32 [48, 64], P('tensor', 'dp')
- grad_down_weight: float32 [3072, 768], P('tensor', 'dp')
- grad_down_bias: float32 [768], P(('dp', 'tensor'))
- grad_second_gain: float32 [768], P(('dp', 'tensor'))
- grad_second_shift: float32 [768], P(('dp', 'tensor'))
All inputs are finite; a program needn't handle non-finite values.
Results may differ from a plain program's by a relative error of at most 0.014.
Values may be sent and summed in bfloat16 or wider, within the bound.
No kernel may reach another device: no remote copies, remote signals or barrier semaphores. Data moves between devices by JAX's collectives and lax.ppermute only.
A program may use at most 192 MiB of HBM per device.

v0:
```python
import math

import jax
import jax.numpy as jnp
from jax import lax
from jax.sharding import PartitionSpec as P

HD = 64
L = 1024


EPSILON = 1e-12


def split_up(array, dim, peers):
    before, after = (array.shape[:dim], array.shape[dim + 1 :])
    return jnp.moveaxis(array.reshape(*before, peers, -1, *after), dim, 0)


def summed_on_arrival(array, axis, dim):
    peers = lax.axis_size(axis)
    parts = lax.all_to_all(split_up(array, dim, peers), axis, 0, 0, tiled=True)
    return jnp.sum(parts.astype(jnp.float32), axis=0)


def layer_norm(residual, norm_gain, norm_shift):
    average = jnp.mean(residual, axis=-1, keepdims=True)
    centered = residual - average
    variance = jnp.mean(centered * centered, axis=-1, keepdims=True)
    inverse = lax.rsqrt(variance + EPSILON)
    normed = centered * inverse
    return (normed * norm_gain + norm_shift, normed, inverse)


def norm_backward(upstream, norm_gain, normed, inverse):
    scaled = upstream * norm_gain
    first_mean = jnp.mean(scaled, axis=-1, keepdims=True)
    second_mean = jnp.mean(scaled * normed, axis=-1, keepdims=True)
    return inverse * (scaled - first_mean - normed * second_mean)


def matmul(left, right):
    return jnp.dot(left, right, preferred_element_type=jnp.float32)


def contract_rows(left, right):
    return lax.dot_general(
        left, right, (((0,), (0,)), ((), ())), preferred_element_type=jnp.float32
    )


def contract_cols(left, right):
    return lax.dot_general(
        left, right, (((1,), (1,)), ((), ())), preferred_element_type=jnp.float32
    )


def exact_gelu(values_in):
    return jax.nn.gelu(values_in, approximate=False)


def by_heads(matrix, seq_count, heads_local):
    return matrix.reshape(seq_count, L, heads_local, HD)


def attend_forward(packed):
    query_seq, key_seq, value_seq = packed
    scaling = 1.0 / math.sqrt(query_seq.shape[-1])
    scores = (
        jnp.einsum("qhd,khd->hqk", query_seq, key_seq, preferred_element_type=jnp.float32) * scaling
    )
    largest = jnp.max(scores, axis=-1, keepdims=True)
    log_total = largest + jnp.log(jnp.sum(jnp.exp(scores - largest), axis=-1, keepdims=True))
    softmax_low = jnp.exp(scores - log_total).astype(jnp.bfloat16)
    context = jnp.einsum("hqk,khd->qhd", softmax_low, value_seq, preferred_element_type=jnp.float32)
    return (context, log_total)


def attend_backward(packed):
    query_seq, key_seq, value_seq, log_total, context_grad = packed
    scaling = 1.0 / math.sqrt(query_seq.shape[-1])
    scores = (
        jnp.einsum("qhd,khd->hqk", query_seq, key_seq, preferred_element_type=jnp.float32) * scaling
    )
    softmax_full = jnp.exp(scores - log_total)
    softmax_low = softmax_full.astype(jnp.bfloat16)
    value_grad = jnp.einsum(
        "hqk,qhd->khd", softmax_low, context_grad, preferred_element_type=jnp.float32
    )
    weight_grad = jnp.einsum(
        "qhd,khd->hqk", context_grad, value_seq, preferred_element_type=jnp.float32
    )
    row_terms = jnp.sum(weight_grad * softmax_full, axis=-1, keepdims=True)
    score_grad = (softmax_full * (weight_grad - row_terms)).astype(jnp.bfloat16)
    query_grad = (
        jnp.einsum("hqk,khd->qhd", score_grad, key_seq, preferred_element_type=jnp.float32)
        * scaling
    )
    key_grad = (
        jnp.einsum("hqk,qhd->khd", score_grad, query_seq, preferred_element_type=jnp.float32)
        * scaling
    )
    return (query_grad, key_grad, value_grad)


def forward(inputs):
    (
        tokens,
        query_weight,
        key_weight,
        value_weight,
        output_weight,
        query_bias,
        value_bias,
        output_bias,
        first_gain,
        first_shift,
        up_weight,
        up_bias,
        down_weight,
        down_bias,
        second_gain,
        second_shift,
    ) = inputs
    attention_set = (
        lax.all_gather(query_weight, "dp", axis=0, tiled=True),
        lax.all_gather(key_weight, "dp", axis=0, tiled=True),
        lax.all_gather(value_weight, "dp", axis=0, tiled=True),
        lax.all_gather(output_weight, "dp", axis=1, tiled=True),
        lax.all_gather(query_bias, "dp", axis=1, tiled=True),
        lax.all_gather(value_bias, "dp", axis=1, tiled=True),
    )
    feedforward_set = (
        lax.all_gather(up_weight, "dp", axis=0, tiled=True),
        lax.all_gather(down_weight, "dp", axis=1, tiled=True),
        lax.all_gather(up_bias, "dp", axis=1, tiled=True),
    )
    vector_set = (
        lax.all_gather(output_bias, ("dp", "tensor"), axis=0, tiled=True),
        lax.all_gather(first_gain, ("dp", "tensor"), axis=0, tiled=True),
        lax.all_gather(first_shift, ("dp", "tensor"), axis=0, tiled=True),
        lax.all_gather(down_bias, ("dp", "tensor"), axis=0, tiled=True),
        lax.all_gather(second_gain, ("dp", "tensor"), axis=0, tiled=True),
        lax.all_gather(second_shift, ("dp", "tensor"), axis=0, tiled=True),
    )
    full_query, full_key, full_value, full_output, full_query_bias, full_value_bias = attention_set
    full_up, full_down, full_up_bias = feedforward_set
    bias_output, gain_first, shift_first, bias_down, gain_second, shift_second = vector_set
    grouped = lax.all_gather(tokens, "tensor", axis=0, tiled=True)
    heads_local = full_query.shape[1] // HD
    seq_count = grouped.shape[0] // L
    queries = (
        matmul(grouped, full_query) + full_query_bias.reshape(-1).astype(jnp.float32)
    ).astype(jnp.bfloat16)
    keys_low = matmul(grouped, full_key).astype(jnp.bfloat16)
    values_low = (
        matmul(grouped, full_value) + full_value_bias.reshape(-1).astype(jnp.float32)
    ).astype(jnp.bfloat16)
    context, log_totals = lax.map(
        attend_forward,
        (
            by_heads(queries, seq_count, heads_local),
            by_heads(keys_low, seq_count, heads_local),
            by_heads(values_low, seq_count, heads_local),
        ),
    )
    context_low = context.astype(jnp.bfloat16).reshape(grouped.shape[0], -1)
    attended = lax.psum_scatter(
        matmul(context_low, full_output), "tensor", scatter_dimension=0, tiled=True
    )
    first_out, normed_first, inverse_first = layer_norm(
        tokens.astype(jnp.float32) + (attended + bias_output), gain_first, shift_first
    )
    hidden_grouped = lax.all_gather(first_out.astype(jnp.bfloat16), "tensor", axis=0, tiled=True)
    pre_activation = matmul(hidden_grouped, full_up) + full_up_bias.reshape(-1).astype(jnp.float32)
    activated = exact_gelu(pre_activation).astype(jnp.bfloat16)
    branch = lax.psum_scatter(
        matmul(activated, full_down), "tensor", scatter_dimension=0, tiled=True
    )
    layer_out, normed_second, inverse_second = layer_norm(
        first_out + (branch + bias_down), gain_second, shift_second
    )
    return (
        layer_out,
        normed_second,
        inverse_second,
        normed_first,
        inverse_first,
        gain_first,
        gain_second,
        grouped,
        queries,
        keys_low,
        values_low,
        log_totals,
        context_low,
        hidden_grouped,
        pre_activation,
        activated,
        full_query,
        full_key,
        full_value,
        full_output,
        full_up,
        full_down,
    )


def local(
    tokens,
    query_weight,
    key_weight,
    value_weight,
    output_weight,
    query_bias,
    value_bias,
    output_bias,
    first_gain,
    first_shift,
    up_weight,
    up_bias,
    down_weight,
    down_bias,
    second_gain,
    second_shift,
    cotangent,
):
    inputs = (
        tokens,
        query_weight,
        key_weight,
        value_weight,
        output_weight,
        query_bias,
        value_bias,
        output_bias,
        first_gain,
        first_shift,
        up_weight,
        up_bias,
        down_weight,
        down_bias,
        second_gain,
        second_shift,
    )
    kept_values = forward(inputs)
    layer_out = kept_values[0]
    inputs_again, cotangent = lax.optimization_barrier((inputs, cotangent))
    kept_values = forward(inputs_again)
    (
        unused_out,
        normed_second,
        inverse_second,
        normed_first,
        inverse_first,
        gain_first,
        gain_second,
        grouped,
        queries,
        keys_low,
        values_low,
        log_totals,
        context_low,
        hidden_grouped,
        pre_activation,
        activated,
        full_query,
        full_key,
        full_value,
        full_output,
        full_up,
        full_down,
    ) = kept_values
    heads_local = full_query.shape[1] // HD
    seq_count = grouped.shape[0] // L
    group_rows = grouped.shape[0]
    upstream = cotangent.astype(jnp.float32)
    grad_second_gain = jnp.sum(upstream * normed_second, axis=0)
    grad_second_shift = jnp.sum(upstream, axis=0)
    error_second = norm_backward(upstream, gain_second, normed_second, inverse_second)
    grad_down_bias = jnp.sum(error_second, axis=0)
    branch_grouped = lax.all_gather(error_second.astype(jnp.bfloat16), "tensor", axis=0, tiled=True)
    grad_down = contract_rows(activated, branch_grouped)
    grad_activated = contract_cols(branch_grouped, full_down)
    unused_value, gelu_back = jax.vjp(exact_gelu, pre_activation)
    grad_pre = gelu_back(grad_activated)[0]
    grad_up_bias = jnp.sum(grad_pre, axis=0).reshape(-1, HD)
    grad_pre_low = grad_pre.astype(jnp.bfloat16)
    grad_up = contract_rows(hidden_grouped, grad_pre_low)
    back_hidden = lax.psum_scatter(
        contract_cols(grad_pre_low, full_up), "tensor", scatter_dimension=0, tiled=True
    )
    error_input = error_second + back_hidden
    grad_first_gain = jnp.sum(error_input * normed_first, axis=0)
    grad_first_shift = jnp.sum(error_input, axis=0)
    error_first = norm_backward(error_input, gain_first, normed_first, inverse_first)
    grad_output_bias = jnp.sum(error_first, axis=0)
    attended_grouped = lax.all_gather(
        error_first.astype(jnp.bfloat16), "tensor", axis=0, tiled=True
    )
    grad_output = contract_rows(context_low, attended_grouped)
    context_grad = contract_cols(attended_grouped, full_output).astype(jnp.bfloat16)
    query_grads, key_grads, value_grads = lax.map(
        attend_backward,
        (
            by_heads(queries, seq_count, heads_local),
            by_heads(keys_low, seq_count, heads_local),
            by_heads(values_low, seq_count, heads_local),
            log_totals,
            by_heads(context_grad, seq_count, heads_local),
        ),
    )
    query_grads = query_grads.reshape(group_rows, -1)
    key_grads = key_grads.reshape(group_rows, -1)
    value_grads = value_grads.reshape(group_rows, -1)
    grad_query_bias = jnp.sum(query_grads, axis=0).reshape(heads_local, HD)
    grad_value_bias = jnp.sum(value_grads, axis=0).reshape(heads_local, HD)
    query_low = query_grads.astype(jnp.bfloat16)
    key_low = key_grads.astype(jnp.bfloat16)
    value_low = value_grads.astype(jnp.bfloat16)
    grad_query = contract_rows(grouped, query_low)
    grad_key = contract_rows(grouped, key_low)
    grad_value = contract_rows(grouped, value_low)
    token_terms = (
        contract_cols(query_low, full_query)
        + contract_cols(key_low, full_key)
        + contract_cols(value_low, full_value)
    )
    grad_tokens = error_first + lax.psum_scatter(
        token_terms.astype(jnp.bfloat16), "tensor", scatter_dimension=0, tiled=True
    ).astype(jnp.float32)
    out_query, out_key, out_value, out_output, out_query_bias, out_value_bias = (
        lax.psum_scatter(grad_query, "dp", scatter_dimension=0, tiled=True),
        lax.psum_scatter(grad_key, "dp", scatter_dimension=0, tiled=True),
        lax.psum_scatter(grad_value, "dp", scatter_dimension=0, tiled=True),
        lax.psum_scatter(grad_output, "dp", scatter_dimension=1, tiled=True),
        lax.psum_scatter(grad_query_bias, "dp", scatter_dimension=1, tiled=True),
        lax.psum_scatter(grad_value_bias, "dp", scatter_dimension=1, tiled=True),
    )
    out_up, out_down, out_up_bias = (
        summed_on_arrival(grad_up.astype(jnp.bfloat16), "dp", 0),
        summed_on_arrival(grad_down.astype(jnp.bfloat16), "dp", 1),
        summed_on_arrival(grad_up_bias.astype(jnp.bfloat16), "dp", 1),
    )
    (
        out_output_bias,
        out_first_gain,
        out_first_shift,
        out_down_bias,
        out_second_gain,
        out_second_shift,
    ) = (
        lax.psum_scatter(grad_output_bias, ("dp", "tensor"), scatter_dimension=0, tiled=True),
        lax.psum_scatter(grad_first_gain, ("dp", "tensor"), scatter_dimension=0, tiled=True),
        lax.psum_scatter(grad_first_shift, ("dp", "tensor"), scatter_dimension=0, tiled=True),
        lax.psum_scatter(grad_down_bias, ("dp", "tensor"), scatter_dimension=0, tiled=True),
        lax.psum_scatter(grad_second_gain, ("dp", "tensor"), scatter_dimension=0, tiled=True),
        lax.psum_scatter(grad_second_shift, ("dp", "tensor"), scatter_dimension=0, tiled=True),
    )
    return (
        layer_out.astype(jnp.bfloat16),
        grad_tokens,
        out_query,
        out_key,
        out_value,
        out_output,
        out_query_bias,
        out_value_bias,
        out_output_bias,
        out_first_gain,
        out_first_shift,
        out_up,
        out_up_bias,
        out_down,
        out_down_bias,
        out_second_gain,
        out_second_shift,
    )


def solution(mesh):
    placed = (
        P(("dp", "tensor"), None),
        P("dp", "tensor"),
        P("dp", "tensor"),
        P("dp", "tensor"),
        P("tensor", "dp"),
        P("tensor", "dp"),
        P("tensor", "dp"),
        P(("dp", "tensor")),
        P(("dp", "tensor")),
        P(("dp", "tensor")),
        P("dp", "tensor"),
        P("tensor", "dp"),
        P("tensor", "dp"),
        P(("dp", "tensor")),
        P(("dp", "tensor")),
        P(("dp", "tensor")),
        P(("dp", "tensor"), None),
    )
    return jax.shard_map(
        local,
        mesh=mesh,
        in_specs=placed,
        out_specs=(
            P(("dp", "tensor"), None),
            P(("dp", "tensor"), None),
            P("dp", "tensor"),
            P("dp", "tensor"),
            P("dp", "tensor"),
            P("tensor", "dp"),
            P("tensor", "dp"),
            P("tensor", "dp"),
            P(("dp", "tensor")),
            P(("dp", "tensor")),
            P(("dp", "tensor")),
            P("dp", "tensor"),
            P("tensor", "dp"),
            P("tensor", "dp"),
            P(("dp", "tensor")),
            P(("dp", "tensor")),
            P(("dp", "tensor")),
        ),
        check_vma=False,
    )
```

profile of v0, /device:TPU:0, one launch (start us, length us, event | category | flops | bytes accessed | tf_op | source)
XLA Modules:
  0.0 1703.4 jit_solution(16481985174851587209)
XLA Ops:
  51.7 33.1 %all_gather.128 = bf16[192,768]{0,1:T(8,128)(2,1)} all-gather(bf16[192,96]{0,1:T(8,128)(2,1)S(1)} %copy.156), channel_id=1, replica_groups=mesh['dp'=8,'tensor'=4] {'dp'}, dimensions={1}, use_global_device_ids=true | all-gather | bytes 331776 | tf_op jit(solution)/shard_map/all_gather | solution.py:129
  84.7 33.1 %all_gather.123 = bf16[768,192]{1,0:T(8,128)(2,1)} all-gather(bf16[96,192]{1,0:T(8,128)(2,1)S(1)} %copy-done.36), channel_id=1, replica_groups=mesh['dp'=8,'tensor'=4] {'dp'}, dimensions={0}, use_global_device_ids=true | all-gather | bytes 331776 | tf_op jit(solution)/shard_map/all_gather | solution.py:128
  117.8 31.2 %all_gather.125 = bf16[768,192]{1,0:T(8,128)(2,1)S(1)} all-gather(bf16[96,192]{1,0:T(8,128)(2,1)S(1)} %copy-done.32), channel_id=1, replica_groups=mesh['dp'=8,'tensor'=4] {'dp'}, dimensions={0}, use_global_device_ids=true | all-gather | bytes 331776 | tf_op jit(solution)/shard_map/all_gather | solution.py:126
  149.1 31.0 %all_gather.127 = bf16[768,192]{1,0:T(8,128)(2,1)S(1)} all-gather(bf16[96,192]{1,0:T(8,128)(2,1)S(1)} %copy-done.34), channel_id=1, replica_groups=mesh['dp'=8,'tensor'=4] {'dp'}, dimensions={0}, use_global_device_ids=true | all-gather | bytes 331776 | tf_op jit(solution)/shard_map/all_gather | solution.py:127
  206.9 35.9 %while.40 = (s32[]{:T(128)}, bf16[4,1024,3,64]{1,3,2,0:T(8,128)(2,1)}, f32[4,3,1024,1]{2,1,3,0:T(4,128)}, bf16[4,1024,3,64]{1,3,2,0:T(8,128)(2,1)}, bf16[4,1024,...) while((s32[]{:T(128)}, bf16[4,1024,3,64]{1,3,2,0:T(8,128)(2,1)}, ...), condition=%wide.region_13.14_spmd.clone, body=%wide.region_10.13_spmd.sunk.clone | while | flops 830469120 | bytes 52406408 | solution.py:159
  256.6 38.9 %all-reduce.20 = (f32[768]{0:T(1024)S(1)}, f32[768]{0:T(1024)S(1)}, f32[768]{0:T(1024)S(1)}, f32[768]{0:T(1024)S(1)}, f32[768]{0:T(1024)S(1)}) all-reduce(f32[768]{0:T(1024)S(1)} %dynamic-update-slice.6, f32[768]{0:T(1024)S(1)} %dynamic-update-slice.8, ...), channel_id=1, replica_groups=mesh['dp'=8,'tensor'=4] {'dp','tensor'}, use_global_device_ids=true, to_apply=%add.6 | all-reduce | flops 3840 | bytes 30720
  295.5 57.8 %reduce-scatter.19.cloned.1.call-done = f32[1024,768]{1,0:T(8,128)} async-done(((f32[4096,768]{1,0:T(8,128)}), f32[1024,768]{1,0:T(8,128)}) %reduce-scatter.19.cloned.1.call-update) | async-done | bytes 3145744 | tf_op jit(solution)/shard_map/reduce_scatter | solution.py:168
  404.7 35.2 %multiply_convert_fusion.1 = (bf16[4096,768]{1,0:T(8,128)(2,1)}, f32[4096,768]{1,0:T(8,128)}, f32[4096,768]{1,0:T(8,128)}) fusion(f32[768]{0:T(1024)S(1)} %reshape.261, bf16[4096,768]{1,0:T(8,128)(2,1)} %all-gather.25.cloned.1.call-done, bf16[768,768]{1,0:T(8,128)(2,1)} %all-gather.27.cloned.1.call-done), kind=kOutput, calls=%fused_computation.79 | convolution fusion | flops 5039456256 | bytes 38931456 | tf_op jit(solution)/shard_map/dot_general | solution.py:43
  458.6 97.5 %reduce-scatter.21.cloned.1.call-done = f32[1024,768]{1,0:T(8,128)} async-done(((f32[4096,768]{1,0:T(8,128)}), f32[1024,768]{1,0:T(8,128)}) %reduce-scatter.21.cloned.1.call-update) | async-done | bytes 3145744 | tf_op jit(solution)/shard_map/reduce_scatter | solution.py:177
  566.8 46.5 %all-gather.31.cloned.1.call-done = bf16[4096,768]{1,0:T(8,128)(2,1)} async-done(((bf16[1024,768]{1,0:T(8,128)(2,1)}), bf16[4096,768]{1,0:T(8,128)(2,1)}) %all-gather.31.cloned.1.call-update) | async-done | bytes 6291472 | tf_op jit(solution)/shard_map/all_gather | solution.py:282
  643.2 99.0 %reduce-scatter.23.cloned.1.call-done = f32[1024,768]{1,0:T(8,128)} async-done(((f32[4096,768]{1,0:T(8,128)}), f32[1024,768]{1,0:T(8,128)}) %reduce-scatter.23.cloned.1.call-update) | async-done | bytes 3145744 | tf_op jit(solution)/shard_map/reduce_scatter | solution.py:290
  752.7 43.2 %all-gather.33.cloned.1.call-done = bf16[4096,768]{1,0:T(8,128)(2,1)} async-done(((bf16[1024,768]{1,0:T(8,128)(2,1)}), bf16[4096,768]{1,0:T(8,128)(2,1)}) %all-gather.33.cloned.1.call-update) | async-done | bytes 6291472 | tf_op jit(solution)/shard_map/all_gather | solution.py:298
  809.9 98.4 %while.41 = (s32[]{:T(128)}, f32[4,1024,3,64]{1,3,2,0:T(8,128)}, bf16[4,1024,3,64]{1,3,2,0:T(8,128)(2,1)}, f32[4,1024,3,64]{1,3,2,0:T(8,128)}, bf16[4,1024,3,64]...) while((s32[]{:T(128)}, f32[4,1024,3,64]{1,3,2,0:T(8,128)}, ...), condition=%wide.region_27.28_spmd.clone, body=%wide.region_25.27_spmd.sunk.clone | while | flops 2051404800 | bytes 124740744 | solution.py:303
  982.4 33.1 %all_gather.108 = bf16[768,192]{1,0:T(8,128)(2,1)} all-gather(bf16[96,192]{1,0:T(8,128)(2,1)S(1)} %copy-done.33), channel_id=1, replica_groups=mesh['dp'=8,'tensor'=4] {'dp'}, dimensions={0}, use_global_device_ids=true | all-gather | bytes 331776 | tf_op jit(solution)/shard_map/all_gather | solution.py:126
  1015.5 31.4 %all_gather.110 = bf16[768,192]{1,0:T(8,128)(2,1)S(1)} all-gather(bf16[96,192]{1,0:T(8,128)(2,1)S(1)} %copy-done.35), channel_id=1, replica_groups=mesh['dp'=8,'tensor'=4] {'dp'}, dimensions={0}, use_global_device_ids=true | all-gather | bytes 331776 | tf_op jit(solution)/shard_map/all_gather | solution.py:127
  1046.9 31.1 %all_gather.106 = bf16[768,192]{1,0:T(8,128)(2,1)S(1)} all-gather(bf16[96,192]{1,0:T(8,128)(2,1)S(1)} %copy-done.37), channel_id=1, replica_groups=mesh['dp'=8,'tensor'=4] {'dp'}, dimensions={0}, use_global_device_ids=true | all-gather | bytes 331776 | tf_op jit(solution)/shard_map/all_gather | solution.py:128
  1078.0 33.0 %all_gather.111 = bf16[192,768]{0,1:T(8,128)(2,1)} all-gather(bf16[192,96]{0,1:T(8,128)(2,1)S(1)} %copy.148), channel_id=1, replica_groups=mesh['dp'=8,'tensor'=4] {'dp'}, dimensions={1}, use_global_device_ids=true | all-gather | bytes 331776 | tf_op jit(solution)/shard_map/all_gather | solution.py:129
  1141.3 29.6 %while.39 = (s32[]{:T(128)}, bf16[4,1024,3,64]{1,3,2,0:T(8,128)(2,1)S(1)}, bf16[4,1024,3,64]{1,3,2,0:T(8,128)(2,1)S(1)}, bf16[4,1024,3,64]{1,3,2,0:T(8,128)(2,1)}, bf16[4,1024,3,64]{1,3,2,0:T(8,128)(2,1)}) while((s32[]{:T(128)}, bf16[4,1024,3,64]{1,3,2,0:T(8,128)(2,1)S(1)}, bf16[4,1024,3,64]{1,3,2,0:T(8,128)(2,1)S(1)}, ...), condition=%wide.region_3.4_spmd.clone, body=%wide.region_0.3_spmd.sunk.clone | while | flops 830469120 | bytes 39807044 | solution.py:159
  1187.6 39.0 %all-reduce.19 = (f32[768]{0:T(1024)S(1)}, f32[768]{0:T(1024)S(1)}, f32[768]{0:T(1024)S(1)}, f32[768]{0:T(1024)}, f32[768]{0:T(1024)}, /*index=5*/f32[768]{0:T(1...) all-reduce(f32[768]{0:T(1024)S(1)} %dynamic-update-slice.2, ...), channel_id=1, replica_groups=mesh['dp'=8,'tensor'=4] {'dp','tensor'}, use_global_device_ids=true, to_apply=%add.2 | all-reduce | flops 9216 | bytes 73728
  1226.6 50.5 %reduce-scatter.15.cloned.1.call-done = f32[1024,768]{1,0:T(8,128)} async-done(((f32[4096,768]{1,0:T(8,128)}), f32[1024,768]{1,0:T(8,128)}) %reduce-scatter.15.cloned.1.call-update) | async-done | bytes 3145744 | tf_op jit(solution)/shard_map/reduce_scatter | solution.py:168
  1329.5 40.3 %fusion.77 = f32[4096,768]{1,0:T(8,128)} fusion(bf16[768,768]{0,1:T(8,128)(2,1)} %all-gather.21.cloned.1.call-done, f32[768]{0:T(1024)S(1)} %reshape.258, bf16[4096,768]{1,0:T(8,128)(2,1)} %all-gather.17.cloned.1.call-done, bf16[768,768]{1,0:T(8,128)(2,1)} %all-gather.19.cloned.1.call-done), kind=kOutput, calls=%fused_computation.108 | convolution fusion | flops 9871294464 | bytes 21236736 | tf_op jit(solution)/shard_map/dot_general | solution.py:43
  1504.0 60.4 %reduce-scatter.31.cloned.1.call-done = f32[96,192]{1,0:T(8,128)} async-done(((f32[768,192]{1,0:T(8,128)}), f32[96,192]{1,0:T(8,128)}) %reduce-scatter.31.cloned.1.call-update) | async-done | bytes 73744 | tf_op jit(solution)/shard_map/reduce_scatter | solution.py:335
  1564.3 65.8 %reduce-scatter.27.cloned.1.call-done = f32[96,192]{1,0:T(8,128)} async-done(((f32[768,192]{1,0:T(8,128)}), f32[96,192]{1,0:T(8,128)}) %reduce-scatter.27.cloned.1.call-update) | async-done | bytes 73744 | tf_op jit(solution)/shard_map/reduce_scatter | solution.py:333
  1630.2 65.3 %reduce-scatter.29.cloned.1.call-done = f32[96,192]{1,0:T(8,128)} async-done(((f32[768,192]{1,0:T(8,128)}), f32[96,192]{1,0:T(8,128)}) %reduce-scatter.29.cloned.1.call-update) | async-done | bytes 73744 | tf_op jit(solution)/shard_map/reduce_scatter | solution.py:334
  (432 shorter events, 688.2 us)
Async XLA Ops:
  8.0 141.0 %copy-start.34 = (bf16[96,192]{1,0:T(8,128)(2,1)S(1)}, bf16[96,192]{1,0:T(8,128)(2,1)}, u32[]{:S(2)}) copy-start(bf16[96,192]{1,0:T(8,128)(2,1)} %param.25) | copy-start | bytes 110596
  8.1 172.0 %all-gather.23.cloned.1.call-start = ((), (), s32[]{:S(2)}) async-start(), calls=%async_computation.19 | async-start | bytes 7864320 | tf_op jit(solution)/shard_map/all_gather | solution.py:149
  8.8 344.5 %reduce-scatter.19.cloned.1.call-start = ((), (), s32[]{:S(2)}) async-start(), calls=%async_computation.20 | async-start | bytes 15728640 | tf_op jit(solution)/shard_map/reduce_scatter | solution.py:168
  254.8 130.4 %all-gather.27.cloned.1.call-start = ((), (), s32[]{:S(2)}) async-start(), calls=%async_computation.22 | async-start | bytes 1327104 | tf_op jit(solution)/shard_map/all_gather | solution.py:134
  255.4 149.3 %all-gather.25.cloned.1.call-start = ((), (), s32[]{:S(2)}) async-start(), calls=%async_computation.21 | async-start | bytes 7864320 | tf_op jit(solution)/shard_map/all_gather | solution.py:174
  358.3 90.0 %all-gather.29.cloned.1.call-start = ((), (), s32[]{:S(2)}) async-start(), calls=%async_computation.23 | async-start | bytes 1327104 | tf_op jit(solution)/shard_map/all_gather | solution.py:135
  358.9 197.2 %reduce-scatter.21.cloned.1.call-start = ((), (), s32[]{:S(2)}) async-start(), calls=%async_computation.24 | async-start | bytes 15728640 | tf_op jit(solution)/shard_map/reduce_scatter | solution.py:177
  458.6 154.7 %all-gather.31.cloned.1.call-start = ((), (), s32[]{:S(2)}) async-start(), calls=%async_computation.25 | async-start | bytes 7864320 | tf_op jit(solution)/shard_map/all_gather | solution.py:282
  566.7 175.5 %reduce-scatter.23.cloned.1.call-start = ((), (), s32[]{:S(2)}) async-start(), calls=%async_computation.26 | async-start | bytes 15728640 | tf_op jit(solution)/shard_map/reduce_scatter | solution.py:290
  643.2 152.7 %all-gather.33.cloned.1.call-start = ((), (), s32[]{:S(2)}) async-start(), calls=%async_computation.27 | async-start | bytes 7864320 | tf_op jit(solution)/shard_map/all_gather | solution.py:298
  749.4 361.6 %all-gather.15.cloned.1.call-start = ((), (), s32[]{:S(2)}) async-start(), calls=%async_computation.13 | async-start | bytes 7864320 | tf_op jit(solution)/shard_map/all_gather | solution.py:149
  749.9 432.1 %reduce-scatter.25.cloned.1.call-start = ((), (), s32[]{:S(2)}) async-start(), calls=%async_computation.28 | async-start | bytes 7864320 | tf_op jit(solution)/shard_map/reduce_scatter | solution.py:329
  944.9 332.2 %reduce-scatter.15.cloned.1.call-start = ((), (), s32[]{:S(2)}) async-start(), calls=%async_computation.14 | async-start | bytes 15728640 | tf_op jit(solution)/shard_map/reduce_scatter | solution.py:168
  1179.3 136.7 %all-gather.19.cloned.1.call-start = ((), (), s32[]{:S(2)}) async-start(), calls=%async_computation.16 | async-start | bytes 1327104 | tf_op jit(solution)/shard_map/all_gather | solution.py:134
  1180.0 136.0 %all-gather.21.cloned.1.call-start = ((), (), s32[]{:S(2)}) async-start(), calls=%async_computation.17 | async-start | bytes 1327104 | tf_op jit(solution)/shard_map/all_gather | solution.py:135
  1180.6 148.9 %all-gather.17.cloned.1.call-start = ((), (), s32[]{:S(2)}) async-start(), calls=%async_computation.15 | async-start | bytes 7864320 | tf_op jit(solution)/shard_map/all_gather | solution.py:174
  1283.2 200.5 %reduce-scatter.33.cloned.1.call-start = ((), (), s32[]{:S(2)}) async-start(), calls=%async_computation.32 | async-start | bytes 884736
  1315.7 182.3 %reduce-scatter.17.cloned.1.call-start = ((), (), s32[]{:S(2)}) async-start(), calls=%async_computation.18 | async-start | bytes 15728640 | tf_op jit(solution)/shard_map/reduce_scatter | solution.py:177
  1371.3 15.6 all-to-all-start.1
  1386.9 34.4 %all-to-all-start.2 = ((bf16[8,768,96]{1,2,0:T(8,128)(2,1)}), bf16[8,768,96]{1,2,0:T(8,128)(2,1)S(1)}, u32[]{:S(2)}, u32[]{:S(2)}) async-start(bf16[8,768,96]{1,2,0:T(8,128)(2,1)} %bitcast.37), calls=%async_computation.11 | async-start | bytes 2359296 | tf_op jit(solution)/shard_map/all_to_all | solution.py:22
  1422.3 32.6 %all-to-all-start = ((bf16[8,96,768]{2,1,0:T(8,128)(2,1)}), bf16[8,96,768]{2,1,0:T(8,128)(2,1)}, u32[]{:S(2)}, u32[]{:S(2)}) async-start(bf16[8,96,768]{2,1,0:T(8,128)(2,1)} %bitcast.287), calls=%async_computation.9 | async-start | bytes 2359296 | tf_op jit(solution)/shard_map/all_to_all | solution.py:22
  1426.6 137.7 %reduce-scatter.31.cloned.1.call-start = ((), (), s32[]{:S(2)}) async-start(), calls=%async_computation.31 | async-start | bytes 884736 | tf_op jit(solution)/shard_map/reduce_scatter | solution.py:335
  1433.0 197.2 %reduce-scatter.27.cloned.1.call-start = ((), (), s32[]{:S(2)}) async-start(), calls=%async_computation.29 | async-start | bytes 884736 | tf_op jit(solution)/shard_map/reduce_scatter | solution.py:333
  1440.0 255.6 %reduce-scatter.29.cloned.1.call-start = ((), (), s32[]{:S(2)}) async-start(), calls=%async_computation.30 | async-start | bytes 884736 | tf_op jit(solution)/shard_map/reduce_scatter | solution.py:334
  (85 other events, 1496.5 us)
Sparse Core Ops, SparseCore 0:
  10.5 49.0 all-gather.22
  254.9 98.2 reduce-scatter.18
  566.9 46.3 all-gather.30
  749.5 46.3 all-gather.32
  797.3 46.3 all-gather.14
  945.0 57.9 reduce-scatter.24
  1179.3 97.6 reduce-scatter.14
Sparse Core Ops, SparseCore 1:
  257.5 40.0 all-gather.26
  358.4 46.2 all-gather.24
  406.7 41.5 all-gather.28
  458.6 97.4 reduce-scatter.20
  643.3 98.9 reduce-scatter.22
  1182.2 39.5 all-gather.18
  1223.8 39.7 all-gather.20
  1283.3 46.1 all-gather.16
  1333.0 62.4 reduce-scatter.32
  1398.1 99.9 reduce-scatter.16
  1501.8 62.5 reduce-scatter.30
  1568.6 61.5 reduce-scatter.26
  1633.9 61.5 reduce-scatter.28
where the time goes:
time: 1710 us; the launch traced here: 1700 us
  waiting for transfers between devices  667 us (39%)
  blocking collectives  482 us (28%)
  matrix products  350 us (20%)
  other arithmetic  88.9 us (5%)
  local copies, waits for them, and re-layouts  79.3 us (5%)
  between operations  17.8 us (1%)
    dot_general x11, matrix products, matmul(): return jnp.dot(left, right, preferred_element_type=jnp.float32)  131 us
    reduce_scatter x2, waiting for transfers between devices, forward(): lax.psum_scatter(matmul(context_low, full_output), 'tensor', scatter_dime...  108 us
    reduce_scatter x2, waiting for transfers between devices, forward(): lax.psum_scatter(matmul(activated, full_down), 'tensor', scatter_dimensio...  103 us
    reduce_scatter x1, waiting for transfers between devices, local(): lax.psum_scatter(contract_cols(grad_pre_low, full_up), 'tensor', scatter_...  99 us
    unnamed x3, blocking collectives  97.5 us
    all_gather x2, blocking collectives, forward(): lax.all_gather(output_weight, 'dp', axis=1, tiled=True)  66 us
    reduce_scatter x1, waiting for transfers between devices, local(): lax.psum_scatter(grad_query, 'dp', scatter_dimension=0, tiled=True)  65.8 us
    reduce_scatter x1, waiting for transfers between devices, local(): lax.psum_scatter(grad_key, 'dp', scatter_dimension=0, tiled=True)  65.3 us
  transfers between devices with their start and end apart: 23, of which 15 were waited for; matrix products, arithmetic and copies ran while one was open for 22% of the time, Pallas kernels for 0%

commit v1 on v0

v1 whole, which is shorter than its diff:
```python
import math

import jax
import jax.numpy as jnp
from jax import lax
from jax.sharding import PartitionSpec as P

HD = 64
L = 1024
EPSILON = 1e-12
AXES = ("dp", "tensor")
EXTRA = 16
BF = jnp.bfloat16
F32 = jnp.float32


def partner(device, stage, bits):
    if stage == "core":
        return device ^ 1
    if stage == "a":
        return device ^ (2 if device & 1 else 4)
    if stage == "b":
        return device ^ (4 if device & 1 else 2)
    return device ^ (1 << stage)


def exchange(array, stage, count):
    bits = count.bit_length() - 1
    return lax.ppermute(array, AXES, [(d, partner(d, stage, bits)) for d in range(count)])


def stages_of(count):
    bits = count.bit_length() - 1
    return [*range(bits - 1, 2, -1), "a", "b", "core"]


def gather_blocks(block, count):
    held = block[None]
    for stage in stages_of(count):
        held = jnp.concatenate([held, exchange(held, stage, count)], axis=0)
    return held


def scatter_blocks(blocks, count):
    for stage in reversed(stages_of(count)):
        half = blocks.shape[0] // 2
        arrived = exchange(blocks[half:], stage, count)
        total = blocks[:half].astype(F32) + arrived.astype(F32)
        blocks = total if half == 1 else total.astype(BF)
    return blocks[0]


def position_table(me, count):
    bits = count.bit_length() - 1
    device = jnp.arange(count, dtype=jnp.int32)
    differs = device ^ me
    one, two = (differs >> 1) & 1, (differs >> 2) & 1
    odd = (device & 1) == 1
    place = ((differs & 1) << (bits - 1)) | (jnp.where(odd, two, one) << (bits - 2))
    place = place | (jnp.where(odd, one, two) << (bits - 3))
    for k in range(3, bits):
        place = place | (((differs >> k) & 1) << (bits - 1 - k))
    return place


def three_parts(vector):
    high = lax.reduce_precision(vector, 8, 7)
    middle = lax.reduce_precision(vector - high, 8, 7)
    lowest = lax.reduce_precision(vector - high - middle, 8, 7)
    return jnp.stack([high, middle, lowest]).astype(BF)


def matmul(left, right):
    return jnp.dot(left, right, preferred_element_type=F32)


def contract_rows(left, right):
    return lax.dot_general(left, right, (((0,), (0,)), ((), ())), preferred_element_type=F32)


def contract_cols(left, right):
    return lax.dot_general(left, right, (((1,), (1,)), ((), ())), preferred_element_type=F32)


def layer_norm(residual, gain, shift):
    average = jnp.mean(residual, axis=-1, keepdims=True)
    centered = residual - average
    variance = jnp.mean(centered * centered, axis=-1, keepdims=True)
    inverse = lax.rsqrt(variance + EPSILON)
    normed = centered * inverse
    return normed * gain + shift, normed, inverse


def norm_backward(upstream, gain, normed, inverse):
    scaled = upstream * gain
    first_mean = jnp.mean(scaled, axis=-1, keepdims=True)
    second_mean = jnp.mean(scaled * normed, axis=-1, keepdims=True)
    return inverse * (scaled - first_mean - normed * second_mean)


def local(
    tokens, query_weight, key_weight, value_weight, output_weight, query_bias, value_bias,
    output_bias, first_gain, first_shift, up_weight, up_bias, down_weight, down_bias,
    second_gain, second_shift, cotangent,
):
    dp, tensor = lax.axis_size("dp"), lax.axis_size("tensor")
    count = dp * tensor
    rows = query_weight.shape[0]
    width = rows * dp
    groups = query_weight.shape[1] // HD
    heads = groups * tensor
    hidden_block = up_weight.shape[1]
    slot = output_bias.shape[0]
    place = position_table(lax.axis_index(AXES), count)
    vectors = jnp.stack([output_bias, first_gain, first_shift, down_bias, second_gain, second_shift])
    small = jnp.concatenate([
        three_parts(vectors).reshape(-1), query_bias.reshape(-1), value_bias.reshape(-1), up_bias.reshape(-1),
    ])
    extra = jnp.pad(small, (0, EXTRA * 4 * HD - small.shape[0])).reshape(EXTRA, 4 * HD)
    output_turned = output_weight.T
    by_group = [
        jnp.concatenate([w[:, c * HD : (c + 1) * HD] for w in (query_weight, key_weight, value_weight, output_turned)], axis=1)
        for c in range(groups)
    ]
    first_set = gather_blocks(jnp.concatenate([by_group[0], extra], axis=0), count)
    second_set = gather_blocks(jnp.concatenate(by_group[1:], axis=1), count)
    up_set = gather_blocks(up_weight, count)
    down_set = gather_blocks(down_weight.T, count)

    def whole(blocks):
        ordered = jnp.take(blocks, place, axis=0)
        return ordered.reshape(dp, tensor, rows, -1).transpose(1, 0, 2, 3).reshape(tensor, width, -1)

    packs = [whole(first_set[:, :rows])]
    rest = whole(second_set)
    packs += [rest[:, :, 4 * HD * c : 4 * HD * (c + 1)] for c in range(groups - 1)]
    up_all = whole(up_set)
    down_all = whole(down_set)
    small_all = jnp.take(first_set[:, rows:].reshape(count, -1), place, axis=0).astype(F32)
    triples = small_all[:, : 18 * slot].reshape(count, 3, 6, slot)
    vectors_all = (triples[:, 0] + triples[:, 1] + triples[:, 2]).transpose(1, 0, 2).reshape(6, width)
    bias_output, gain_first, shift_first, bias_down, gain_second, shift_second = vectors_all

    def biases(start, size):
        block = small_all[:, start : start + size].reshape(dp, tensor, -1, HD // dp)
        return block.transpose(1, 2, 0, 3).reshape(-1, HD)

    at = 18 * slot
    query_bias_all = biases(at, query_bias.size)
    value_bias_all = biases(at + query_bias.size, value_bias.size)
    up_bias_all = biases(at + 2 * query_bias.size, up_bias.size).reshape(tensor, hidden_block)

    sequences = tokens.shape[0] // L
    scale = 1.0 / math.sqrt(HD)
    pre = jnp.concatenate([matmul(tokens, packs[c][t][:, : 3 * HD])[None] for t in range(tensor) for c in range(groups)])
    pre = pre.reshape(heads, sequences, L, 3 * HD)
    queries = (pre[..., :HD] + query_bias_all[:, None, None]).astype(BF)
    keys = pre[..., HD : 2 * HD].astype(BF)
    values = (pre[..., 2 * HD :] + value_bias_all[:, None, None]).astype(BF)
    scores = jnp.einsum("hsqd,hskd->hsqk", queries, keys, preferred_element_type=F32) * scale
    probs = jax.nn.softmax(scores, axis=-1).astype(BF)
    context = jnp.einsum("hsqk,hskd->hsqd", probs, values, preferred_element_type=F32).astype(BF)
    context_flat = context.transpose(1, 2, 0, 3).reshape(-1, width)
    output_all = jnp.concatenate([packs[c][t][:, 3 * HD :] for t in range(tensor) for c in range(groups)], axis=1)
    attended = contract_cols(context_flat, output_all)
    first_out, normed_first, inverse_first = layer_norm(tokens.astype(F32) + (attended + bias_output), gain_first, shift_first)
    hidden = first_out.astype(BF)
    pre_act = jnp.stack([matmul(hidden, up_all[t]) + up_bias_all[t] for t in range(tensor)])
    act = jax.nn.gelu(pre_act, approximate=False).astype(BF)
    branch = sum(contract_cols(act[t], down_all[t]) for t in range(tensor))
    layer_out, normed_second, inverse_second = layer_norm(first_out + (branch + bias_down), gain_second, shift_second)

    upstream = cotangent.astype(F32)
    grad_second_gain = jnp.sum(upstream * normed_second, axis=0)
    grad_second_shift = jnp.sum(upstream, axis=0)
    err_two = norm_backward(upstream, gain_second, normed_second, inverse_second)
    grad_down_bias = jnp.sum(err_two, axis=0)
    err_two_low = err_two.astype(BF)

    def blocks_of(parts):
        stacked = jnp.stack(parts).reshape(tensor, dp, rows, -1).transpose(1, 0, 2, 3).reshape(count, rows, -1)
        return jnp.zeros_like(stacked).at[place].set(stacked)

    grad_down = scatter_blocks(blocks_of([contract_rows(err_two_low, act[t]).astype(BF) for t in range(tensor)]), count)
    grad_act = jnp.stack([matmul(err_two_low, down_all[t]) for t in range(tensor)])
    grad_pre = jax.vjp(lambda v: jax.nn.gelu(v, approximate=False), pre_act)[1](grad_act)[0]
    grad_up_bias = jnp.sum(grad_pre, axis=1)
    grad_pre_low = grad_pre.astype(BF)
    grad_up = scatter_blocks(blocks_of([contract_rows(hidden, grad_pre_low[t]).astype(BF) for t in range(tensor)]), count)
    err_in = err_two + sum(contract_cols(grad_pre_low[t], up_all[t]) for t in range(tensor))
    grad_first_gain = jnp.sum(err_in * normed_first, axis=0)
    grad_first_shift = jnp.sum(err_in, axis=0)
    err_one = norm_backward(err_in, gain_first, normed_first, inverse_first)
    grad_output_bias = jnp.sum(err_one, axis=0)
    err_one_low = err_one.astype(BF)
    context_grad = matmul(err_one_low, output_all).astype(BF).reshape(sequences, L, heads, HD).transpose(2, 0, 1, 3)
    grad_values = jnp.einsum("hsqk,hsqd->hskd", probs, context_grad, preferred_element_type=F32)
    dprobs = jnp.einsum("hsqd,hskd->hsqk", context_grad, values, preferred_element_type=F32)
    row_terms = jnp.sum(context_grad.astype(F32) * context.astype(F32), axis=-1, keepdims=True)
    dscores = (probs.astype(F32) * (dprobs - row_terms)).astype(BF)
    grad_queries = jnp.einsum("hsqk,hskd->hsqd", dscores, keys, preferred_element_type=F32) * scale
    grad_keys = jnp.einsum("hsqk,hsqd->hskd", dscores, queries, preferred_element_type=F32) * scale
    grad_query_bias = jnp.sum(grad_queries, axis=(1, 2))
    grad_value_bias = jnp.sum(grad_values, axis=(1, 2))
    triple = jnp.concatenate([grad_queries, grad_keys, grad_values], axis=-1).astype(BF).reshape(heads, -1, 3 * HD)
    context_rows = context.reshape(heads, -1, HD)

    def head_grad(h):
        return jnp.concatenate([contract_rows(tokens, triple[h]), contract_rows(err_one_low, context_rows[h])], axis=1).astype(BF)

    second_grad = scatter_blocks(blocks_of([
        jnp.concatenate([head_grad(t * groups + c) for c in range(1, groups)], axis=1) for t in range(tensor)
    ]), count)
    grad_tokens = err_one + sum(
        contract_cols(triple[t * groups + c], packs[c][t][:, : 3 * HD]) for t in range(tensor) for c in range(groups)
    )
    vector_grads = jnp.stack([
        grad_output_bias, grad_first_gain, grad_first_shift, grad_down_bias, grad_second_gain, grad_second_shift,
    ]).reshape(6, count, slot).transpose(1, 0, 2).reshape(count, -1)

    def bias_blocks(bias):
        return bias.reshape(tensor, -1, dp, HD // dp).transpose(2, 0, 1, 3).reshape(count, -1)

    small_grads = jnp.concatenate([
        vector_grads, bias_blocks(grad_query_bias), bias_blocks(grad_value_bias), bias_blocks(grad_up_bias.reshape(-1, HD)),
    ], axis=1)
    high = lax.reduce_precision(small_grads, 8, 7)
    small_grads = high
    small_grads = jnp.pad(small_grads, ((0, 0), (0, EXTRA * 4 * HD - small_grads.shape[1]))).astype(BF)
    small_grads = jnp.zeros_like(small_grads).at[place].set(small_grads).reshape(count, EXTRA, 4 * HD)
    first_grad = scatter_blocks(
        jnp.concatenate([blocks_of([head_grad(t * groups) for t in range(tensor)]), small_grads], axis=1), count
    )
    packed = jnp.concatenate([first_grad[:rows], second_grad], axis=1).reshape(rows, groups, 4, HD)
    out_query, out_key, out_value, out_output = (packed[:, :, i].reshape(rows, groups * HD) for i in range(4))
    tail = first_grad[rows:].reshape(-1)
    vecs = tail[: 6 * slot].reshape(6, slot)
    bias_at = 6 * slot
    return (
        layer_out.astype(BF),
        grad_tokens,
        out_query,
        out_key,
        out_value,
        out_output.T,
        tail[bias_at : bias_at + slot].reshape(query_bias.shape),
        tail[bias_at + slot : bias_at + 2 * slot].reshape(value_bias.shape),
        vecs[0],
        vecs[1],
        vecs[2],
        grad_up,
        tail[bias_at + 2 * slot : bias_at + 2 * slot + up_bias.size].reshape(up_bias.shape),
        grad_down.T,
        vecs[3],
        vecs[4],
        vecs[5],
    )


def solution(mesh):
    both, cross, turned, vector = P(AXES, None), P("dp", "tensor"), P("tensor", "dp"), P(AXES)
    return jax.shard_map(
        local,
        mesh=mesh,
        in_specs=(
            both, cross, cross, cross, turned, turned, turned, vector, vector, vector,
            cross, turned, turned, vector, vector, vector, both,
        ),
        out_specs=(
            both, both, cross, cross, cross, turned, turned, turned, vector, vector, vector,
            cross, turned, turned, vector, vector, vector,
        ),
        check_vma=False,
    )
```

time: 1710 us -> 755 us (0.44)
  waiting for transfers between devices: 667 us -> 69 us
  blocking collectives: 482 us -> 0 us
  local copies, waits for them, and re-layouts: 79.3 us -> 235 us
  matrix products: 350 us -> 259 us
  other arithmetic: 88.9 us -> 132 us
  starting transfers between devices: 17 us -> 43 us
    reduce_scatter x9 -> x0, waiting for transfers between devices: 501 us -> none  [the longest x2 108 us: forward(): lax.psum_scatter(matmul(context_low, full_output), 'tensor', scatter_dime...]
    all_gather x14 -> x0, blocking collectives: 384 us -> none  [the longest x2 66 us: forward(): lax.all_gather(output_weight, 'dp', axis=1, tiled=True)]
    all_gather x10 -> x0, waiting for transfers between devices: 131 us -> none  [the longest x1 46.5 us: local(): lax.all_gather(error_second.astype(jnp.bfloat16), 'tensor', axis=0, tiled...]
    dot_general x47 -> x26, matrix products: 246 us -> 117 us  [the longest x21 40.6 us: matmul(): return jnp.dot(left, right, preferred_element_type=F32)]
    unnamed x3 -> x0, blocking collectives: 97.5 us -> none
    ppermute x0 -> x40, waiting for transfers between devices: none -> 69 us  [exchange(): lax.ppermute(array, AXES, [(d, partner(d, stage, bits)) for d in range(co...]
    slice x0 -> x54, local copies, waits for them, and re-layouts: none -> 47 us  [the longest x20 13.4 us: scatter_blocks(): arrived = exchange(blocks[half:], stage, count)]
    concatenate x0 -> x36, local copies, waits for them, and re-layouts: none -> 46.3 us  [the longest x24 25.5 us: head_grad(): jnp.concatenate([contract_rows(tokens, triple[h]), contract_rows(err_one_...]
  transfers between devices with their start and end apart: 23 -> 40, of which waited for: 15 -> 15; matrix products, arithmetic and copies ran while one was open for 22% -> 48% of each run, Pallas kernels for 0% -> 0%
where the time goes in v1:
time: 755 us; the launch traced here: 741 us
  matrix products  259 us (34%)
  local copies, waits for them, and re-layouts  235 us (31%)
  other arithmetic  132 us (17%)
  waiting for transfers between devices  69 us (9%)
  starting transfers between devices  43 us (6%)
    ppermute x40, waiting for transfers between devices, exchange(): lax.ppermute(array, AXES, [(d, partner(d, stage, bits)) for d in range(co...  69 us
    dot_general x21, matrix products, contract_cols(): lax.dot_general(left, right, (((1,), (1,)), ((), ())), preferred_element_...  67.4 us
    dot_general x32, matrix products, contract_rows(): lax.dot_general(left, right, (((0,), (0,)), ((), ())), preferred_element_...  51.6 us
    ppermute x40, starting transfers between devices, exchange(): lax.ppermute(array, AXES, [(d, partner(d, stage, bits)) for d in range(co...  43 us
    dot_general x21, matrix products, matmul(): return jnp.dot(left, right, preferred_element_type=F32)  40.6 us
    scatter x4, local copies, waits for them, and re-layouts, blocks_of(): return jnp.zeros_like(stacked).at[place].set(stacked)  36.1 us
    unnamed x294, local copies, waits for them, and re-layouts  36 us
    convert_element_type x1, other arithmetic, local(): act = jax.nn.gelu(pre_act, approximate=False).astype(BF)  27.8 us
  transfers between devices with their start and end apart: 40, of which 15 were waited for; matrix products, arithmetic and copies ran while one was open for 48% of the time, Pallas kernels for 0%

profile of v1, /device:TPU:0, one launch (start us, length us, event | category | flops | bytes accessed | tf_op | source)
XLA Modules:
  0.0 741.0 jit_solution(7236813268104896759)
XLA Ops:
  71.3 9.1 %collective-permute-done.12 = bf16[4,96,768]{2,1,0:T(8,128)(2,1)S(1)} collective-permute-done((bf16[4,96,768]{2,1,0:T(8,128)(2,1)S(1)}, bf16[4,96,768]{2,1,0:T(8,128)(2,1)S(1)}, u32[]{:S(2)}, u32[]{:S(2)}) %collective-permute-start.12) | collective-permute-done | bytes 589856 | tf_op jit(solution)/shard_map/ppermute | solution.py:29
  182.0 23.8 %fusion.156 = (f32[12,1024]{1,0:T(8,128)S(1)}, f32[12,1024,1024]{1,2,0:T(8,128)}) fusion(f32[12,1,1024,192]{2,3,0,1:T(8,128)} %bitcast.555, f32[12,64]{1,0:T(8,128)} %add.310), kind=kOutput, calls=%fused_computation.425 | convolution fusion | flops 1649935360 | bytes 55107584 | tf_op jit(solution)/shard_map/sub | solution.py:161
  205.8 26.3 %divide_convert_fusion = bf16[12,1024,1024]{1,2,0:T(8,128)(2,1)} fusion(f32[12,1024,1024]{1,2,0:T(8,128)} %get-tuple-element.228, f32[12,1024]{1,0:T(8,128)S(1)} %get-tuple-element.227), kind=kLoop, calls=%fused_computation.12 | loop fusion | flops 25165824 | bytes 75546624 | tf_op jit(solution)/shard_map/convert_element_type | solution.py:161
  232.1 13.8 %convolution_convert_fusion = bf16[12,1024,64]{1,2,0:T(8,128)(2,1)S(1)} fusion(bf16[12,1024,1024]{1,2,0:T(8,128)(2,1)} %divide_convert_fusion, f32[12,1,1024,192]{2,3,0,1:T(8,128)} %bitcast.556, f32[12,64]{1,0:T(8,128)S(1)} %add.313), kind=kOutput, calls=%fused_computation.92 | convolution fusion | flops 1612972032 | bytes 29887488 | tf_op jit(solution)/shard_map/hsqk,hskd->hsqd/dot_general | solution.py:162
  265.4 5.5 gather_fusion.4
  274.1 5.5 gather_fusion.3
  279.7 6.9 broadcast_select_fusion.1
  297.8 27.8 %multiply_convert_fusion.1 = (bf16[4,1024,768]{2,1,0:T(8,128)(2,1)S(1)}, f32[4,1024,768]{2,1,0:T(8,128)S(1)}) fusion(f32[1,1024,768]{2,1,0:T(8,128)S(1)} %add_bitcast_fusion, f32[1,1024,768]{2,1,0:T(8,128)S(1)} %add_bitcast_fusion.1, f32[1,1024,768]{2,1,0:T(8,128)S(1)} %add_bitcast_fusion.2, f32[1,1024,768]{2,1,0:T(8,128)S(1)} %add_bitcast_fusion.3), kind=kLoop, calls=%fused_computation.22 | loop fusion | flops 213909504 | bytes 31457280 | tf_op jit(solution)/shard_map/convert_element_type | solution.py:169
  335.4 5.6 fusion.162
  368.5 12.1 %fusion.140 = (f32[4,768]{1,0:T(4,128)S(1)}, bf16[4,1024,768]{2,1,0:T(8,128)(2,1)}) fusion(f32[4,1024,768]{2,1,0:T(8,128)S(1)} %get-tuple-element.117, f32[1,1024,768]{2,1,0:T(8,128)} %convolution_bitcast_fusion, f32[1,1024,768]{2,1,0:T(8,128)} %convolution_bitcast_fusion.1, f32[1,1024,768]{2,1,0:T(8,128)} %convolution_bitcast_fusion.2, ...), kind=kLoop, calls=%fused_computation.410 | loop fusion | flops 66057216 | bytes 44052480 | tf_op jit(solution)/shard_map/reduce_sum | solution.py:187
  411.3 13.9 %fusion.144 = (f32[12,64]{1,0:T(8,128)S(1)}, bf16[12,1,1024,64]{2,3,0,1:T(8,128)(2,1)}) fusion(bf16[12,1024,1024]{1,2,0:T(8,128)(2,1)} %divide_convert_fusion, bf16[12,1024,64]{1,2,0:T(8,128)(2,1)} %bitcast.566), kind=kOutput, calls=%fused_computation.413 | convolution fusion | flops 1612184832 | bytes 28314624 | tf_op jit(solution)/shard_map/hsqk,hsqd->hskd/dot_general | solution.py:197
  425.2 19.4 %multiply_convert_fusion = bf16[12,1024,1024]{1,2,0:T(8,128)(2,1)} fusion(bf16[12,1024,1024]{1,2,0:T(8,128)(2,1)} %divide_convert_fusion, f32[12,1024]{1,0:T(8,128)S(1)} %multiply_reduce_fusion.2, bf16[12,1024,64]{1,2,0:T(8,128)(2,1)} %bitcast.567, f32[12,1,1024,192]{2,3,0,1:T(8,128)} %bitcast.557, f32[12,64]{1,0:T(8,128)S(1)} %add.313), kind=kOutput, calls=%fused_computation.11 | convolution fusion | flops 1662517248 | bytes 55102464 | tf_op jit(solution)/shard_map/hsqd,hskd->hsqk/dot_general | solution.py:198
  444.6 14.7 %multiply_reduce_fusion.6 = (f32[12,64]{1,0:T(8,128)S(1)}, bf16[12,1,1024,64]{2,3,0,1:T(8,128)(2,1)}) fusion(bf16[12,1024,1024]{1,2,0:T(8,128)(2,1)} %multiply_convert_fusion, f32[12,1,1024,192]{2,3,0,1:T(8,128)} %bitcast.558), kind=kOutput, calls=%fused_computation.79 | convolution fusion | flops 1612971264 | bytes 28314624 | tf_op jit(solution)/shard_map/hsqk,hskd->hsqd/dot_general | solution.py:201
  459.3 14.3 %fusion.27 = bf16[12,1,1024,64]{2,3,0,1:T(8,128)(2,1)} fusion(bf16[12,1024,1024]{1,2,0:T(8,128)(2,1)} %multiply_convert_fusion, f32[12,1,1024,192]{2,3,0,1:T(8,128)} %bitcast.559, f32[12,64]{1,0:T(8,128)S(1)} %copy-done.114), kind=kOutput, calls=%fused_computation.118 | convolution fusion | flops 1613758464 | bytes 29887488 | tf_op jit(solution)/shard_map/hsqk,hsqd->hskd/dot_general | solution.py:202
  521.0 12.0 %scatter_fusion.3 = bf16[32,96,768]{2,1,0:T(8,128)(2,1)} fusion(bf16[32,96,768]{2,1,0:T(8,128)(2,1)} %broadcast.468.clone.1, s32[32]{0:T(128)S(1)} %copy-done.113, bf16[32,96,768]{2,1,0:T(8,128)(2,1)} %bitcast.552), kind=kCustom, calls=%fused_computation.9 | custom fusion | bytes 14155904 | tf_op jit(solution)/shard_map/scatter | solution.py:182
  543.0 12.1 %scatter_fusion.2 = bf16[32,96,768]{2,1,0:T(8,128)(2,1)} fusion(bf16[32,96,768]{2,1,0:T(8,128)(2,1)} %broadcast.468.clone, s32[32]{0:T(128)S(1)} %copy-done.113, bf16[32,96,768]{2,1,0:T(8,128)(2,1)} %bitcast.553), kind=kCustom, calls=%fused_computation.8 | custom fusion | bytes 14155904 | tf_op jit(solution)/shard_map/scatter | solution.py:182
  606.6 6.6 maximum_maximum_fusion
  615.2 10.3 %scatter_fusion.1 = bf16[32,96,512]{2,1,0:T(8,128)(2,1)} fusion(bf16[32,96,512]{2,1,0:T(8,128)(2,1)} %broadcast_in_dim.136, s32[32]{0:T(128)S(1)} %copy-done.113, bf16[32,96,512]{2,1,0:T(8,128)(2,1)} %bitcast.562), kind=kCustom, calls=%fused_computation.7 | custom fusion | bytes 9437312 | tf_op jit(solution)/shard_map/scatter | solution.py:182
  640.9 11.0 %add_add_fusion = f32[1024,768]{0,1:T(8,128)} fusion(f32[1024,768]{0,1:T(8,128)S(1)} %copy-done.6, f32[1024,768]{0,1:T(8,128)} %fusion.82, f32[1024,768]{0,1:T(8,128)} %fusion.81, f32[1024,768]{0,1:T(8,128)} %fusion.80, f32[1024,768]{0,1:T(8,128)} %fusion.79, f32[1024,768]{0,1:T(8,128)} %fusion.78, f32[1024,768]{0,1:T(8,128)} %fusion.77, ...), kind=kOutput, calls=%fused_computation.62 | convolution fusion | flops 311427072 | bytes 41680896 | tf_op jit(solution)/shard_map/dot_general | solution.py:82
  668.9 5.6 collective-permute-done.26
  680.3 6.6 collective-permute-done.27
  688.2 4.8 collective-permute-done.28
  695.2 16.1 %collective-permute-done.31 = bf16[8,96,768]{2,1,0:T(8,128)(2,1)S(1)} collective-permute-done((bf16[8,96,768]{2,1,0:T(8,128)(2,1)S(1)}, bf16[8,96,768]{2,1,0:T(8,128)(2,1)S(1)}, u32[]{:S(2)}, u32[]{:S(2)}) %collective-permute-start.31) | collective-permute-done | bytes 1179680 | tf_op jit(solution)/shard_map/ppermute | solution.py:29
  716.1 6.5 collective-permute-done.32
  (661 shorter events, 447.8 us)
Async XLA Ops:
  3.6 25.0 %collective-permute-start.5 = (bf16[1,96,512]{2,1,0:T(8,128)(2,1)S(1)}, bf16[1,96,512]{2,1,0:T(8,128)(2,1)}, u32[]{:S(2)}, u32[]{:S(2)}) collective-permute-start(bf16[1,96,512]{2,1,0:T(8,128)(2,1)S(1)} %bitcast.586), channel_id=1, source_target_pairs={{0,16},{1,17},{2,18},{3,19},{4,20},{5,21},{6,22},{7,23},{8,24},{9,... | collective-permute-start | bytes 294920 | tf_op jit(solution)/shard_map/ppermute | solution.py:29
  11.9 20.4 %collective-permute-start.15 = (bf16[1,96,768]{2,1,0:T(8,128)(2,1)}, bf16[1,96,768]{2,1,0:T(8,128)(2,1)}, u32[]{:S(2)}, u32[]{:S(2)}) collective-permute-start(bf16[1,96,768]{2,1,0:T(8,128)(2,1)} %bitcast.590), channel_id=1, source_target_pairs={{0,16},{1,17},{2,18},{3,19},{4,20},{5,21},{6,22},{7,23},{8,24},{9,... | collective-permute-start | bytes 442376 | tf_op jit(solution)/shard_map/ppermute | solution.py:29
  14.8 19.6 %collective-permute-start.10 = (bf16[1,96,768]{2,1,0:T(8,128)(2,1)}, bf16[1,96,768]{2,1,0:T(8,128)(2,1)}, u32[]{:S(2)}, u32[]{:S(2)}) collective-permute-start(bf16[1,96,768]{2,1,0:T(8,128)(2,1)} %bitcast.594), channel_id=1, source_target_pairs={{0,16},{1,17},{2,18},{3,19},{4,20},{5,21},{6,22},{7,23},{8,24},{9,... | collective-permute-start | bytes 442376 | tf_op jit(solution)/shard_map/ppermute | solution.py:29
  33.2 16.0 %collective-permute-start.16 = (bf16[2,96,768]{2,1,0:T(8,128)(2,1)S(1)}, bf16[2,96,768]{2,1,0:T(8,128)(2,1)S(1)}, u32[]{:S(2)}, u32[]{:S(2)}) collective-permute-start(bf16[2,96,768]{2,1,0:T(8,128)(2,1)S(1)} %pad_maximum_fusion.11), channel_id=1, source_target_pairs={{0,8},{1,9},{2,10},{3,11},{4,12},{5,13},{6,14},{7,15},{8,0},{9,1},... | collective-permute-start | bytes 884744 | tf_op jit(solution)/shard_map/ppermute | solution.py:29
  35.3 16.5 %collective-permute-start.11 = (bf16[2,96,768]{2,1,0:T(8,128)(2,1)S(1)}, bf16[2,96,768]{2,1,0:T(8,128)(2,1)S(1)}, u32[]{:S(2)}, u32[]{:S(2)}) collective-permute-start(bf16[2,96,768]{2,1,0:T(8,128)(2,1)S(1)} %pad_maximum_fusion.10), channel_id=1, source_target_pairs={{0,8},{1,9},{2,10},{3,11},{4,12},{5,13},{6,14},{7,15},{8,0},{9,1},... | collective-permute-start | bytes 884744 | tf_op jit(solution)/shard_map/ppermute | solution.py:29
  50.2 17.6 %collective-permute-start.17 = (bf16[4,96,768]{2,1,0:T(8,128)(2,1)S(1)}, bf16[4,96,768]{2,1,0:T(8,128)(2,1)S(1)}, u32[]{:S(2)}, u32[]{:S(2)}) collective-permute-start(bf16[4,96,768]{2,1,0:T(8,128)(2,1)S(1)} %pad_maximum_fusion.7), channel_id=1, source_target_pairs={{0,4},{1,3},{2,6},{3,1},{4,0},{5,7},{6,2},{7,5},{8,12},{9,11},{10,... | collective-permute-start | bytes 1769480 | tf_op jit(solution)/shard_map/ppermute | solution.py:29
  52.8 27.7 %collective-permute-start.12 = (bf16[4,96,768]{2,1,0:T(8,128)(2,1)S(1)}, bf16[4,96,768]{2,1,0:T(8,128)(2,1)S(1)}, u32[]{:S(2)}, u32[]{:S(2)}) collective-permute-start(bf16[4,96,768]{2,1,0:T(8,128)(2,1)S(1)} %pad_maximum_fusion.6), channel_id=1, source_target_pairs={{0,4},{1,3},{2,6},{3,1},{4,0},{5,7},{6,2},{7,5},{8,12},{9,11},{10,... | collective-permute-start | bytes 1769480 | tf_op jit(solution)/shard_map/ppermute | solution.py:29
  56.2 30.1 %collective-permute-start.8 = (bf16[8,96,512]{2,1,0:T(8,128)(2,1)S(1)}, bf16[8,96,512]{2,1,0:T(8,128)(2,1)S(1)}, u32[]{:S(2)}, u32[]{:S(2)}) collective-permute-start(bf16[8,96,512]{2,1,0:T(8,128)(2,1)S(1)} %pad_maximum_fusion.5), channel_id=1, source_target_pairs={{0,2},{1,5},{2,0},{3,7},{4,6},{5,1},{6,4},{7,3},{8,10},{9,13},{10,... | collective-permute-start | bytes 2359304 | tf_op jit(solution)/shard_map/ppermute | solution.py:29
  61.2 26.3 %collective-permute-start.4 = (bf16[16,112,256]{2,1,0:T(8,128)(2,1)S(1)}, bf16[16,112,256]{2,1,0:T(8,128)(2,1)S(1)}, u32[]{:S(2)}, u32[]{:S(2)}) collective-permute-start(bf16[16,112,256]{2,1,0:T(8,128)(2,1)S(1)} %get-tuple-element.158), channel_id=1, source_target_pairs={{0,1},{1,0},{2,3},{3,2},{4,5},{5,4},{6,7},{7,6},{8,9},{9,8},{10,11... | collective-permute-start | bytes 2752520 | tf_op jit(solution)/shard_map/ppermute | solution.py:29
  69.8 77.8 %collective-permute-start.18 = (bf16[8,96,768]{2,1,0:T(8,128)(2,1)}, bf16[8,96,768]{2,1,0:T(8,128)(2,1)}, u32[]{:S(2)}, u32[]{:S(2)}) collective-permute-start(bf16[8,96,768]{2,1,0:T(8,128)(2,1)} %pad_maximum_fusion.4), channel_id=1, source_target_pairs={{0,2},{1,5},{2,0},{3,7},{4,6},{5,1},{6,4},{7,3},{8,10},{9,13},{10,... | collective-permute-start | bytes 3538952 | tf_op jit(solution)/shard_map/ppermute | solution.py:29
  82.5 68.5 %collective-permute-start.13 = (bf16[8,96,768]{2,1,0:T(8,128)(2,1)}, bf16[8,96,768]{2,1,0:T(8,128)(2,1)}, u32[]{:S(2)}, u32[]{:S(2)}) collective-permute-start(bf16[8,96,768]{2,1,0:T(8,128)(2,1)} %pad_maximum_fusion.3), channel_id=1, source_target_pairs={{0,2},{1,5},{2,0},{3,7},{4,6},{5,1},{6,4},{7,3},{8,10},{9,13},{10,... | collective-permute-start | bytes 3538952 | tf_op jit(solution)/shard_map/ppermute | solution.py:29
  87.6 66.4 %collective-permute-start.9 = (bf16[16,96,512]{2,1,0:T(8,128)(2,1)}, bf16[16,96,512]{2,1,0:T(8,128)(2,1)}, u32[]{:S(2)}, u32[]{:S(2)}) collective-permute-start(bf16[16,96,512]{2,1,0:T(8,128)(2,1)} %get-tuple-element.150), channel_id=1, source_target_pairs={{0,1},{1,0},{2,3},{3,2},{4,5},{5,4},{6,7},{7,6},{8,9},{9,8},{10,11... | collective-permute-start | bytes 4718600 | tf_op jit(solution)/shard_map/ppermute | solution.py:29
  150.5 111.6 %collective-permute-start.19 = (bf16[16,96,768]{2,1,0:T(8,128)(2,1)}, bf16[16,96,768]{2,1,0:T(8,128)(2,1)}, u32[]{:S(2)}, u32[]{:S(2)}) collective-permute-start(bf16[16,96,768]{2,1,0:T(8,128)(2,1)} %get-tuple-element.148), channel_id=1, source_target_pairs={{0,1},{1,0},{2,3},{3,2},{4,5},{5,4},{6,7},{7,6},{8,9},{9,8},{10,11... | collective-permute-start | bytes 7077896 | tf_op jit(solution)/shard_map/ppermute | solution.py:29
  154.0 117.0 %collective-permute-start.14 = (bf16[16,96,768]{2,1,0:T(8,128)(2,1)}, bf16[16,96,768]{2,1,0:T(8,128)(2,1)}, u32[]{:S(2)}, u32[]{:S(2)}) collective-permute-start(bf16[16,96,768]{2,1,0:T(8,128)(2,1)} %get-tuple-element.146), channel_id=1, source_target_pairs={{0,1},{1,0},{2,3},{3,2},{4,5},{5,4},{6,7},{7,6},{8,9},{9,8},{10,11... | collective-permute-start | bytes 7077896 | tf_op jit(solution)/shard_map/ppermute | solution.py:29
  536.4 128.1 %collective-permute-start.35 = (bf16[16,96,768]{2,1,0:T(8,128)(2,1)}, bf16[16,96,768]{2,1,0:T(8,128)(2,1)}, u32[]{:S(2)}, u32[]{:S(2)}) collective-permute-start(bf16[16,96,768]{2,1,0:T(8,128)(2,1)} %slice.941), channel_id=1, source_target_pairs={{0,1},{1,0},{2,3},{3,2},{4,5},{5,4},{6,7},{7,6},{8,9},{9,8},{10,11... | collective-permute-start | bytes 7077896 | tf_op jit(solution)/shard_map/ppermute | solution.py:29
  558.4 117.2 %collective-permute-start.30 = (bf16[16,96,768]{2,1,0:T(8,128)(2,1)}, bf16[16,96,768]{2,1,0:T(8,128)(2,1)}, u32[]{:S(2)}, u32[]{:S(2)}) collective-permute-start(bf16[16,96,768]{2,1,0:T(8,128)(2,1)} %slice.930), channel_id=1, source_target_pairs={{0,1},{1,0},{2,3},{3,2},{4,5},{5,4},{6,7},{7,6},{8,9},{9,8},{10,11... | collective-permute-start | bytes 7077896 | tf_op jit(solution)/shard_map/ppermute | solution.py:29
  572.3 32.2 %collective-permute-start.20 = (bf16[16,112,256]{2,1,0:T(8,128)(2,1)}, bf16[16,112,256]{2,1,0:T(8,128)(2,1)}, u32[]{:S(2)}, u32[]{:S(2)}) collective-permute-start(bf16[16,112,256]{2,1,0:T(8,128)(2,1)} %slice.891), channel_id=1, source_target_pairs={{0,1},{1,0},{2,3},{3,2},{4,5},{5,4},{6,7},{7,6},{8,9},{9,8},{10,11... | collective-permute-start | bytes 2752520 | tf_op jit(solution)/shard_map/ppermute | solution.py:29
  605.9 26.7 %collective-permute-start.21 = (bf16[8,112,256]{2,1,0:T(8,128)(2,1)S(1)}, bf16[8,112,256]{2,1,0:T(8,128)(2,1)}, u32[]{:S(2)}, u32[]{:S(2)}) collective-permute-start(bf16[8,112,256]{2,1,0:T(8,128)(2,1)S(1)} %slice.893), channel_id=1, source_target_pairs={{0,2},{1,5},{2,0},{3,7},{4,6},{5,1},{6,4},{7,3},{8,10},{9,13},{10,... | collective-permute-start | bytes 1376264 | tf_op jit(solution)/shard_map/ppermute | solution.py:29
  628.4 31.6 %collective-permute-start.25 = (bf16[16,96,512]{2,1,0:T(8,128)(2,1)}, bf16[16,96,512]{2,1,0:T(8,128)(2,1)}, u32[]{:S(2)}, u32[]{:S(2)}) collective-permute-start(bf16[16,96,512]{2,1,0:T(8,128)(2,1)} %slice.910), channel_id=1, source_target_pairs={{0,1},{1,0},{2,3},{3,2},{4,5},{5,4},{6,7},{7,6},{8,9},{9,8},{10,11... | collective-permute-start | bytes 4718600 | tf_op jit(solution)/shard_map/ppermute | solution.py:29
  640.2 17.1 %collective-permute-start.23 = (bf16[2,112,256]{2,1,0:T(8,128)(2,1)S(1)}, bf16[2,112,256]{2,1,0:T(8,128)(2,1)S(1)}, u32[]{:S(2)}, u32[]{:S(2)}) collective-permute-start(bf16[2,112,256]{2,1,0:T(8,128)(2,1)S(1)} %slice.897), channel_id=1, source_target_pairs={{0,8},{1,9},{2,10},{3,11},{4,12},{5,13},{6,14},{7,15},{8,0},{9,1},... | collective-permute-start | bytes 344072 | tf_op jit(solution)/shard_map/ppermute | solution.py:29
  667.8 25.6 %collective-permute-start.36 = (bf16[8,96,768]{2,1,0:T(8,128)(2,1)S(1)}, bf16[8,96,768]{2,1,0:T(8,128)(2,1)S(1)}, u32[]{:S(2)}, u32[]{:S(2)}) collective-permute-start(bf16[8,96,768]{2,1,0:T(8,128)(2,1)S(1)} %slice.943), channel_id=1, source_target_pairs={{0,2},{1,5},{2,0},{3,7},{4,6},{5,1},{6,4},{7,3},{8,10},{9,13},{10,... | collective-permute-start | bytes 3538952 | tf_op jit(solution)/shard_map/ppermute | solution.py:29
  678.1 33.1 %collective-permute-start.31 = (bf16[8,96,768]{2,1,0:T(8,128)(2,1)S(1)}, bf16[8,96,768]{2,1,0:T(8,128)(2,1)S(1)}, u32[]{:S(2)}, u32[]{:S(2)}) collective-permute-start(bf16[8,96,768]{2,1,0:T(8,128)(2,1)S(1)} %slice.932), channel_id=1, source_target_pairs={{0,2},{1,5},{2,0},{3,7},{4,6},{5,1},{6,4},{7,3},{8,10},{9,13},{10,... | collective-permute-start | bytes 3538952 | tf_op jit(solution)/shard_map/ppermute | solution.py:29
  693.1 19.5 %collective-permute-start.29 = (bf16[1,96,512]{2,1,0:T(8,128)(2,1)S(1)}, bf16[1,96,512]{2,1,0:T(8,128)(2,1)S(1)}, u32[]{:S(2)}, u32[]{:S(2)}) collective-permute-start(bf16[1,96,512]{2,1,0:T(8,128)(2,1)S(1)} %slice.918), channel_id=1, source_target_pairs={{0,16},{1,17},{2,18},{3,19},{4,20},{5,21},{6,22},{7,23},{8,24},{9,... | collective-permute-start | bytes 294920 | tf_op jit(solution)/shard_map/ppermute | solution.py:29
  694.6 18.2 %collective-permute-start.37 = (bf16[4,96,768]{2,1,0:T(8,128)(2,1)}, bf16[4,96,768]{2,1,0:T(8,128)(2,1)}, u32[]{:S(2)}, u32[]{:S(2)}) collective-permute-start(bf16[4,96,768]{2,1,0:T(8,128)(2,1)} %slice.945), channel_id=1, source_target_pairs={{0,4},{1,3},{2,6},{3,1},{4,0},{5,7},{6,2},{7,5},{8,12},{9,11},{10,... | collective-permute-start | bytes 1769480 | tf_op jit(solution)/shard_map/ppermute | solution.py:29
  (145 other events, 1421.4 us)

commit v2 on v1

v2 whole, which is shorter than its diff:
```python
import functools
import math

import jax
import jax.numpy as jnp
import numpy as np
from jax import lax
from jax.experimental import pallas as pl
from jax.experimental.pallas import tpu as pltpu
from jax.sharding import PartitionSpec as P

HD = 64
L = 1024
PACK = 4 * HD
EPSILON = 1e-12
AXES = ("dp", "tensor")
EXTRA = 16
LANES = 128
BF = jnp.bfloat16
F32 = jnp.float32
SDS = jax.ShapeDtypeStruct
ANY = pl.BlockSpec(memory_space=pl.ANY)


def nn(a, b):
    return lax.dot_general(a, b, (((1,), (0,)), ((), ())), preferred_element_type=F32)


def nt(a, b):
    return lax.dot_general(a, b, (((1,), (1,)), ((), ())), preferred_element_type=F32)


def full(shape):
    return pl.BlockSpec(shape, lambda *_: (0,) * len(shape))


def call(body, grid, tables, ins, outs, scratch, cost, name):
    flops, moved = cost
    return pl.pallas_call(
        body,
        grid_spec=pltpu.PrefetchScalarGridSpec(
            num_scalar_prefetch=len(tables),
            grid=grid,
            in_specs=[s for _, s in ins],
            out_specs=[s for _, _, s in outs],
            scratch_shapes=scratch,
        ),
        out_shape=[SDS(s, d) for s, d, _ in outs],
        compiler_params=pltpu.CompilerParams(
            dimension_semantics=("arbitrary",) * len(grid), vmem_limit_bytes=56 * 2**20
        ),
        cost_estimate=pl.CostEstimate(flops=int(flops), bytes_accessed=int(moved), transcendentals=0),
        name=name,
    )(*tables, *[a for a, _ in ins])


def partner(device, stage):
    if stage == "core":
        return device ^ 1
    if stage == "a":
        return device ^ (2 if device & 1 else 4)
    if stage == "b":
        return device ^ (4 if device & 1 else 2)
    return device ^ (1 << stage)


def exchange(array, stage, count):
    return lax.ppermute(array, AXES, [(d, partner(d, stage)) for d in range(count)])


def stages_of(count):
    bits = count.bit_length() - 1
    return [*range(bits - 1, 2, -1), "a", "b", "core"]


def gather_blocks(block, count):
    held = block[None]
    for stage in stages_of(count)[:-2]:
        held = jnp.concatenate([held, exchange(held, stage, count)], axis=0)
    pieces = [held, exchange(held, "b", count)]
    return pieces + [exchange(piece, "core", count) for piece in pieces]


def scatter_blocks(keep, send, count):
    terms = [keep]
    for stage in reversed(stages_of(count)):
        terms.append(exchange(send, stage, count))
        half = terms[-1].shape[0] // 2
        if half:
            send = sum(t[half : 2 * half].astype(F32) for t in terms).astype(BF)
            terms = [t[:half] for t in terms]
    return sum(t[0].astype(F32) for t in terms)


def position_table(me, count):
    bits = count.bit_length() - 1
    device = jnp.arange(count, dtype=jnp.int32)
    differs = device ^ me
    one, two = (differs >> 1) & 1, (differs >> 2) & 1
    odd = (device & 1) == 1
    place = ((differs & 1) << (bits - 1)) | (jnp.where(odd, two, one) << (bits - 2))
    place = place | (jnp.where(odd, one, two) << (bits - 3))
    for k in range(3, bits):
        place = place | (((differs >> k) & 1) << (bits - 1 - k))
    return place


def device_table(me, count):
    bits = count.bit_length() - 1
    place = jnp.arange(count, dtype=jnp.int32)
    core = (place >> (bits - 1)) & 1
    upper, lower = (place >> (bits - 2)) & 1, (place >> (bits - 3)) & 1
    odd = ((me ^ core) & 1) == 1
    one, two = jnp.where(odd, lower, upper), jnp.where(odd, upper, lower)
    differs = core | (one << 1) | (two << 2)
    for k in range(3, bits):
        differs = differs | (((place >> (bits - 1 - k)) & 1) << k)
    return differs ^ me


class Blocks:
    def __init__(self, n, rows, tensor):
        self.n, self.rows, self.tensor = n, rows, tensor

    def at(self, d):
        return lax.rem(d, self.tensor), pl.multiple_of(lax.div(d, self.tensor) * self.rows, self.rows)

    def loads(self, devs, pieces, target, sems, lane=0):
        out, p = [], 0
        width = target.shape[-1]
        for piece in pieces:
            for j in range(piece.shape[0]):
                t, row = self.at(devs[p])
                out.append(pltpu.make_async_copy(
                    piece.at[j, pl.ds(0, self.rows), pl.ds(lane, width)], target.at[t, pl.ds(row, self.rows), :], sems.at[p]
                ))
                p += 1
        return out

    def stores(self, place, t, stage, keep, send, sems, action):
        half = self.n // 2
        for i in range(self.n // self.tensor):
            p = place[i * self.tensor + t]
            source = stage.at[pl.ds(i * self.rows, self.rows), :]
            kept = pltpu.make_async_copy(source, keep.at[lax.rem(p, half), pl.ds(0, self.rows), :], sems.at[i])
            sent = pltpu.make_async_copy(source, send.at[lax.rem(p, half), pl.ds(0, self.rows), :], sems.at[i])
            if action == "wait":
                kept.wait()
            else:
                pl.when(p < half)(kept.start)
                pl.when(p >= half)(sent.start)


def spread_constants(slot, cols, width):
    lane = np.arange(width)
    a, c = np.zeros((LANES, width), np.float32), np.zeros((LANES, width), np.float32)
    for j in range(slot):
        a[j] = lane % slot == j
    for j in range(cols):
        a[32 + j] = lane % cols == j
        c[64 + j] = lane % cols == j
    return jnp.asarray(a, BF), jnp.asarray(c, BF)


def small_masks(device, slot, cols, width, tensor):
    n = device.shape[0]
    shift = tensor.bit_length() - 1
    row = lax.broadcasted_iota(jnp.int32, (n, EXTRA, width), 1)
    lane = lax.broadcasted_iota(jnp.int32, (n, EXTRA, width), 2)
    i, t = device >> shift, device & (tensor - 1)
    in_head = (lane & (HD - 1)) >> (cols.bit_length() - 1)
    groups = width // HD // tensor
    vector = (row < 9) & (lane >= device * slot) & (lane < (device + 1) * slot)
    bias = (row >= 9) & (row < 9 + groups) & ((lane >> 6) == t * groups + row - 9) & (in_head == i)
    hidden = (row < width // HD) & ((lane >> 6) == row) & (in_head == i)
    return vector | bias, hidden, t


def unpack_small(extras, device, slot, cols, width, tensor):
    n = extras.shape[0]
    spread_a, spread_c = spread_constants(slot, cols, width)

    def body(x_ref, d_ref, a_ref, c_ref, vec_ref, bias_ref, up_ref):
        x = x_ref[...].reshape(n * EXTRA, 2 * LANES)
        d = d_ref[...].reshape(n, 1, 1)
        main, hidden, t = small_masks(d, slot, cols, width, tensor)
        for half in range(2):
            y = nn(x[:, half * LANES : (half + 1) * LANES], a_ref[...]).reshape(n, EXTRA, width)
            total = jnp.sum(jnp.where(main, y, 0.0), axis=0)
            for v in range(half, 6, 2):
                r = v // 2
                vec_ref[v : v + 1, :] = total[r : r + 1] + total[3 + r : 4 + r] + total[6 + r : 7 + r]
            bias_ref[half : half + 1, :] = jnp.sum(total[9:EXTRA], axis=0, keepdims=True)
        y = nn(x[:, :LANES], c_ref[...]).reshape(n, EXTRA, width)
        y = jnp.where(hidden, y, 0.0)
        for k in range(tensor):
            picked = jnp.sum(jnp.where(t == k, y, 0.0), axis=0)
            up_ref[k : k + 1, :] = jnp.sum(picked, axis=0, keepdims=True)

    row8 = (8, width)
    return call(
        body, (1,), [],
        [(extras, full(extras.shape)), (device, full(device.shape)), (spread_a, full(spread_a.shape)), (spread_c, full(spread_c.shape))],
        [(row8, F32, full(row8))] * 3, [], (3 * 2 * n * EXTRA * LANES * width, extras.size * 2), "unpack_small",
    )


def pack_small_grads(vec, bias, up, device, slot, cols, tensor):
    n, width = device.shape[0], vec.shape[-1]
    spread_a, spread_c = spread_constants(slot, cols, width)

    def body(v_ref, b_ref, u_ref, d_ref, a_ref, c_ref, out_ref):
        d = d_ref[...].reshape(n, 1, 1)
        main, hidden, t = small_masks(d, slot, cols, width, tensor)
        row = lax.broadcasted_iota(jnp.int32, (EXTRA, width), 0)
        halves = []
        for half in range(2):
            z = jnp.zeros((EXTRA, width), F32)
            for v in range(half, 6, 2):
                z = jnp.where(row == v // 2, v_ref[v : v + 1, :], z)
            z = jnp.where((row >= 9), b_ref[half : half + 1, :], z)
            spread = jnp.where(main, z[None], 0.0).astype(BF).reshape(n * EXTRA, width)
            halves.append(nt(spread, a_ref[...]))
        z = jnp.zeros((n, EXTRA, width), F32)
        for k in range(tensor):
            z = jnp.where(t == k, u_ref[k : k + 1, :].reshape(1, 1, width), z)
        spread = jnp.where(hidden, z, 0.0).astype(BF).reshape(n * EXTRA, width)
        halves[0] = halves[0] + nt(spread, c_ref[...])
        out_ref[...] = jnp.concatenate(halves, axis=1).astype(BF).reshape(n, EXTRA, 2 * LANES)

    shape = (n, EXTRA, PACK)
    return call(
        body, (1,), [],
        [(a, full(a.shape)) for a in (vec, bias, up, device, spread_a, spread_c)],
        [(shape, BF, full(shape))], [], (3 * 2 * n * EXTRA * LANES * width, 2 * n * EXTRA * PACK), "pack_small",
    )[0]


def three_parts(vector):
    high = lax.reduce_precision(vector, 8, 7)
    middle = lax.reduce_precision(vector - high, 8, 7)
    lowest = lax.reduce_precision(vector - high - middle, 8, 7)
    return jnp.stack([high, middle, lowest]).astype(BF)


def small_block(vectors, query_bias, value_bias, up_bias):
    slot = vectors.shape[1]
    parts = three_parts(vectors).reshape(9, 2, slot)

    def placed(array, row, lane):
        return jnp.pad(array, ((row, EXTRA - row - array.shape[0]), (lane, PACK - lane - array.shape[1])))

    return (
        placed(parts[:, 0], 0, 0) + placed(parts[:, 1], 0, LANES) + placed(query_bias, 9, 32)
        + placed(value_bias, 9, LANES + 32) + placed(up_bias, 0, 64)
    )


def attention_forward(tokens, pieces, lane, bias, devs, blocks):
    length, width = tokens.shape
    heads = blocks.tensor
    inner = heads * HD

    def body(devs_ref, x_ref, b_ref, *refs):
        piece_refs, (qkv_ref, e_ref, ctx_ref, ctxt_ref, inv_ref, ot_ref, w, ot_s, sems) = refs[: len(pieces)], refs[len(pieces) :]
        t = pl.program_id(0)

        @pl.when(t == 0)
        def _():
            copies = blocks.loads(devs_ref, piece_refs, w, sems, lane)
            for c in copies:
                c.start()
            for c in copies:
                c.wait()

        wt = w[t]
        pre = nn(x_ref[...], wt)
        b = b_ref[pl.ds(t, 1), :]
        col = lax.broadcasted_iota(jnp.int32, (1, PACK), 1)
        full_rows = (pre + b) * jnp.where(col < HD, 1.0 / math.sqrt(HD), 1.0)
        low = full_rows.astype(BF)
        qkv_ref[0] = low
        q, k = low[:, :HD], low[:, HD : 2 * HD]
        vt = low[:, 2 * HD :].T[:HD]
        scores = nt(k, q)
        e = jnp.exp(scores - jnp.max(scores, axis=0, keepdims=True)).astype(BF)
        e_ref[0] = e
        mixed = nn(jnp.concatenate([vt, jnp.ones((16, length), BF)], axis=0), e)
        inv = 1.0 / mixed[HD : HD + 1]
        inv_ref[0] = jnp.broadcast_to(inv, (8, length))
        ctxt_ref[pl.ds(t * HD, HD), :] = mixed[:HD] * inv
        ot_s[pl.ds(t * HD, HD), :] = wt[:, 2 * HD :].T[HD:].astype(F32)

        @pl.when(t == heads - 1)
        def _():
            ctx_ref[...] = ctxt_ref[...].T.astype(BF)
            ot_ref[...] = ot_s[...].astype(BF)

    by_head = lambda *s: pl.BlockSpec((1, *s), lambda t, *_: (t, 0, 0))
    return call(
        body, (heads,), [devs],
        [(tokens, full(tokens.shape)), (bias, full(bias.shape))] + [(p, ANY) for p in pieces],
        [
            ((heads, length, PACK), BF, by_head(length, PACK)),
            ((heads, length, length), BF, by_head(length, length)),
            ((length, inner), BF, full((length, inner))),
            ((inner, length), F32, full((inner, length))),
            ((heads, 8, length), F32, by_head(8, length)),
            ((inner, width), BF, full((inner, width))),
        ],
        [pltpu.VMEM((heads, width, PACK), BF), pltpu.VMEM((inner, width), F32), pltpu.SemaphoreType.DMA((blocks.n,))],
        (heads * (2 * length * width * PACK + 16 * length * length * HD), heads * length * length * 2), "attention_forward",
    )


def attention_backward(tokens_t, err_t, qkv, e, inv, ctx, ctxt, dctxt, place, blocks, extra):
    width, length = tokens_t.shape
    heads = blocks.tensor
    inner = heads * HD
    half = blocks.n // 2
    scale = 1.0 / math.sqrt(HD)

    def body(place_ref, xt_ref, et_ref, qkv_ref, e_ref, inv_ref, ctx_ref, ctxt_ref, dctxt_ref, keep_ref, send_ref, d_ref, b_ref, stage, go, sems):
        t = pl.program_id(0)

        @pl.when(t == 0)
        def _():
            go[...] = nn(et_ref[...], ctx_ref[...])

        q, k, v = qkv_ref[0, :, :HD], qkv_ref[0, :, HD : 2 * HD], qkv_ref[0, :, 2 * HD : 3 * HD]
        mine = pl.ds(t * HD, HD)
        dot = (dctxt_ref[mine, :].astype(F32) * inv_ref[0, :1, :]).astype(BF)
        delta = jnp.sum(dot.astype(F32) * ctxt_ref[mine, :], axis=0, keepdims=True)
        ee = e_ref[0]
        ds = (ee.astype(F32) * (nn(v, dot) - delta)).astype(BF)
        dv = nn(ee, dot.T)
        dk = nn(ds, q)
        dq = (nn(k.T, ds) * scale).T
        d = jnp.concatenate([dq, dk, dv, jnp.zeros_like(dv)], axis=1)
        b_ref[0] = jnp.broadcast_to(jnp.sum(d, axis=0, keepdims=True), (8, PACK))
        low = d.astype(BF)
        d_ref[0] = low
        slot = lax.rem(t, 2)

        @pl.when(t >= 2)
        def _():
            blocks.stores(place_ref, t - 2, stage.at[slot], keep_ref, send_ref, sems.at[slot], "wait")

        g = nn(xt_ref[...], low)
        for h in range(heads):
            @pl.when(t == h)
            def _():
                stage[slot] = jnp.concatenate([g[:, : 3 * HD], go[:, h * HD : (h + 1) * HD]], axis=1).astype(BF)

        blocks.stores(place_ref, t, stage.at[slot], keep_ref, send_ref, sems.at[slot], "start")

        @pl.when(t == heads - 1)
        def _():
            for last in range(max(heads - 2, 0), heads):
                blocks.stores(place_ref, last, stage.at[last % 2], keep_ref, send_ref, sems.at[last % 2], "wait")

    by_head = lambda *s: pl.BlockSpec((1, *s), lambda t, *_: (t, 0, 0))
    out = (half, blocks.rows + extra, PACK)
    return call(
        body, (heads,), [place],
        [
            (tokens_t, full(tokens_t.shape)), (err_t, full(err_t.shape)), (qkv, by_head(length, PACK)), (e, by_head(length, length)),
            (inv, by_head(8, length)), (ctx, full(ctx.shape)), (ctxt, full(ctxt.shape)), (dctxt, full(dctxt.shape)),
        ],
        [(out, BF, ANY), (out, BF, ANY), ((heads, length, PACK), BF, by_head(length, PACK)), ((heads, 8, PACK), F32, by_head(8, PACK))],
        [pltpu.VMEM((2, width, PACK), BF), pltpu.VMEM((width, inner), F32), pltpu.SemaphoreType.DMA((2, blocks.n // heads))],
        (heads * (2 * length * width * PACK + 32 * length * length * HD), heads * length * length * 2), "attention_backward",
    )


def tokens_backward(err_one, grads, weights, devs, blocks):
    length, width = err_one.shape
    heads = blocks.tensor
    groups = len(grads)
    flat = [p for pieces, _ in weights for p in pieces]

    def body(devs_ref, err_ref, *refs):
        d_refs, piece_refs, (out_ref, w, sems) = refs[:groups], refs[groups : groups + len(flat)], refs[groups + len(flat) :]
        c = pl.program_id(0)

        @pl.when(c == 0)
        def _():
            at, copies = 0, []
            for g, (pieces, lane) in enumerate(weights):
                copies += blocks.loads(devs_ref, piece_refs[at : at + len(pieces)], w.at[g], sems.at[g], lane)
                at += len(pieces)
            for copy in copies:
                copy.start()
            for copy in copies:
                copy.wait()

        total = err_ref[...]
        for g in range(groups):
            for t in range(heads):
                total = total + nt(d_refs[g][t][:, : 3 * HD], w[g, t][:, : 3 * HD])
        out_ref[...] = total

    chunk = min(256, length)
    rows = pl.BlockSpec((chunk, width), lambda c, *_: (c, 0))
    return call(
        body, (length // chunk,), [devs],
        [(err_one, rows)] + [(d, pl.BlockSpec((heads, chunk, PACK), lambda c, *_: (0, c, 0))) for d in grads] + [(p, ANY) for p in flat],
        [((length, width), F32, rows)],
        [pltpu.VMEM((groups, heads, width, PACK), BF), pltpu.SemaphoreType.DMA((groups, blocks.n))],
        (2 * groups * heads * length * width * PACK, groups * heads * width * PACK * 2 + length * width * 8), "tokens_backward",
    )[0]


def layer_norm(residual):
    centered = residual - jnp.mean(residual, axis=-1, keepdims=True)
    inverse = lax.rsqrt(jnp.mean(centered * centered, axis=-1, keepdims=True) + EPSILON)
    return centered * inverse, inverse


def norm_backward(scaled, normed, inverse):
    first = jnp.mean(scaled, axis=-1, keepdims=True)
    second = jnp.mean(scaled * normed, axis=-1, keepdims=True)
    return inverse * (scaled - first - normed * second)


def output_and_up(tokens, contexts, outputs, vec, up_bias, pieces, devs, blocks):
    length, width = tokens.shape
    tensor = blocks.tensor
    hidden_width = tensor * pieces[0].shape[-1]
    part = pieces[0].shape[-1]
    groups = len(contexts)
    chunk = min(256, length)

    def body(devs_ref, x_ref, vec_ref, ub_ref, *refs):
        c_refs, o_refs, piece_refs = refs[:groups], refs[groups : 2 * groups], refs[2 * groups : 2 * groups + len(pieces)]
        norm_ref, inv_ref, hid_ref, hidt_ref, act_ref, slope_ref, w, sems = refs[2 * groups + len(pieces) :]
        c = pl.program_id(0)

        @pl.when(c == 0)
        def _():
            for copy in blocks.loads(devs_ref, piece_refs, w, sems):
                copy.start()

        attended = sum(nn(a[...], b[...]) for a, b in zip(c_refs, o_refs)) + vec_ref[0:1, :]
        normed, inverse = layer_norm(x_ref[...].astype(F32) + attended)
        norm_ref[...] = normed
        inv_ref[...] = inverse
        first_out = normed * vec_ref[1:2, :] + vec_ref[2:3, :]
        hidden = first_out.astype(BF)
        hid_ref[...] = hidden
        hidt_ref[...] = first_out.T.astype(BF)

        @pl.when(c == 0)
        def _():
            for copy in blocks.loads(devs_ref, piece_refs, w, sems):
                copy.wait()

        for t in range(tensor):
            pre = nn(hidden, w[t]) + ub_ref[t : t + 1, :]
            phi = 0.5 * (1.0 + lax.erf(pre * (1.0 / math.sqrt(2.0))))
            act_ref[:, t * part : (t + 1) * part] = (pre * phi).astype(BF)
            density = jnp.exp(-0.5 * pre * pre) * (1.0 / math.sqrt(2.0 * math.pi))
            slope_ref[:, t * part : (t + 1) * part] = (phi + pre * density).astype(BF)

    rows = lambda n: pl.BlockSpec((chunk, n), lambda c, *_: (c, 0))
    cols = lambda n: pl.BlockSpec((n, chunk), lambda c, *_: (0, c))
    return call(
        body, (length // chunk,), [devs],
        [(tokens, rows(width)), (vec, full(vec.shape)), (up_bias, full(up_bias.shape))]
        + [(a, rows(a.shape[1])) for a in contexts] + [(b, full(b.shape)) for b in outputs] + [(p, ANY) for p in pieces],
        [
            ((length, width), F32, rows(width)), ((length, 1), F32, rows(1)), ((length, width), BF, rows(width)),
            ((width, length), BF, cols(width)), ((length, hidden_width), BF, rows(hidden_width)), ((length, hidden_width), BF, rows(hidden_width)),
        ],
        [pltpu.VMEM((tensor, width, part), BF), pltpu.SemaphoreType.DMA((blocks.n,))],
        (2 * length * width * (width + hidden_width), 16 * length * width + 4 * length * hidden_width), "output_and_up",
    )


def down_and_norm(act, normed_one, cotangent, vec, pieces, devs, blocks):
    length, width = normed_one.shape
    tensor = blocks.tensor
    part = pieces[0].shape[-1]
    chunk = min(256, length)

    def body(devs_ref, act_ref, n1_ref, cot_ref, vec_ref, *refs):
        piece_refs, (out_ref, err_ref, errlow_ref, errt_ref, sums_ref, w, sems) = refs[: len(pieces)], refs[len(pieces) :]
        c = pl.program_id(0)

        @pl.when(c == 0)
        def _():
            copies = blocks.loads(devs_ref, piece_refs, w, sems)
            for copy in copies:
                copy.start()
            for copy in copies:
                copy.wait()

        branch = sum(nt(act_ref[:, t * part : (t + 1) * part], w[t]) for t in range(tensor)) + vec_ref[3:4, :]
        first_out = n1_ref[...] * vec_ref[1:2, :] + vec_ref[2:3, :]
        normed, inverse = layer_norm(first_out + branch)
        out_ref[...] = (normed * vec_ref[4:5, :] + vec_ref[5:6, :]).astype(BF)
        upstream = cot_ref[...].astype(F32)
        err = norm_backward(upstream * vec_ref[4:5, :], normed, inverse)
        err_ref[...] = err
        errlow_ref[...] = err.astype(BF)
        errt_ref[...] = err.T.astype(BF)
        rows = [jnp.sum(a, axis=0, keepdims=True) for a in (err, upstream * normed, upstream)]
        sums = jnp.concatenate(rows + [jnp.zeros((5, width), F32)], axis=0)

        @pl.when(c == 0)
        def _():
            sums_ref[...] = sums

        @pl.when(c > 0)
        def _():
            sums_ref[...] += sums

    rows = lambda n: pl.BlockSpec((chunk, n), lambda c, *_: (c, 0))
    return call(
        body, (length // chunk,), [devs],
        [(act, rows(act.shape[1])), (normed_one, rows(width)), (cotangent, rows(width)), (vec, full(vec.shape))] + [(p, ANY) for p in pieces],
        [
            ((length, width), BF, rows(width)), ((length, width), F32, rows(width)), ((length, width), BF, rows(width)),
            ((width, length), BF, pl.BlockSpec((width, chunk), lambda c, *_: (0, c))), ((8, width), F32, full((8, width))),
        ],
        [pltpu.VMEM((tensor, width, part), BF), pltpu.SemaphoreType.DMA((blocks.n,))],
        (2 * length * width * act.shape[1], 2 * act.size + 16 * length * width), "down_and_norm",
    )


def weight_gradient(left_t, right, place, blocks):
    width, length = left_t.shape
    tensor = blocks.tensor
    part = right.shape[1] // tensor

    def body(place_ref, l_ref, r_ref, keep_ref, send_ref, stage, sems):
        t = pl.program_id(0)
        slot = lax.rem(t, 2)

        @pl.when(t >= 2)
        def _():
            blocks.stores(place_ref, t - 2, stage.at[slot], keep_ref, send_ref, sems.at[slot], "wait")

        stage[slot] = nn(l_ref[...], r_ref[...]).astype(BF)
        blocks.stores(place_ref, t, stage.at[slot], keep_ref, send_ref, sems.at[slot], "start")

        @pl.when(t == tensor - 1)
        def _():
            for last in range(max(tensor - 2, 0), tensor):
                blocks.stores(place_ref, last, stage.at[last % 2], keep_ref, send_ref, sems.at[last % 2], "wait")

    out = (blocks.n // 2, blocks.rows, part)
    return call(
        body, (tensor,), [place],
        [(left_t, full(left_t.shape)), (right, pl.BlockSpec((length, part), lambda t, *_: (0, t)))],
        [(out, BF, ANY), (out, BF, ANY)],
        [pltpu.VMEM((2, width, part), BF), pltpu.SemaphoreType.DMA((2, blocks.n // tensor))],
        (2 * length * width * right.shape[1], 2 * (left_t.size + right.size + width * right.shape[1])), "weight_gradient",
    )


def pre_gradient(err_low, slope, pieces, devs, blocks):
    length, width = err_low.shape
    tensor = blocks.tensor
    part = pieces[0].shape[-1]

    def body(devs_ref, e_ref, s_ref, *refs):
        piece_refs, (out_ref, sum_ref, w, sems) = refs[: len(pieces)], refs[len(pieces) :]
        t = pl.program_id(0)

        @pl.when(t == 0)
        def _():
            copies = blocks.loads(devs_ref, piece_refs, w, sems)
            for copy in copies:
                copy.start()
            for copy in copies:
                copy.wait()

        grad = nn(e_ref[...], w[t]) * s_ref[...].astype(F32)
        out_ref[...] = grad.astype(BF)
        sum_ref[pl.ds(t, 1), :] = jnp.sum(grad, axis=0, keepdims=True)

    part_cols = pl.BlockSpec((length, part), lambda t, *_: (0, t))
    return call(
        body, (tensor,), [devs],
        [(err_low, full(err_low.shape)), (slope, part_cols)] + [(p, ANY) for p in pieces],
        [(slope.shape, BF, part_cols), ((8, part), F32, full((8, part)))],
        [pltpu.VMEM((tensor, width, part), BF), pltpu.SemaphoreType.DMA((blocks.n,))],
        (2 * length * width * slope.shape[1], 4 * slope.size + 2 * width * slope.shape[1]), "pre_gradient",
    )


def hidden_gradient(grad_pre, err_two, normed_one, inverse_one, vec, outputs, pieces, devs, blocks):
    length, width = err_two.shape
    tensor = blocks.tensor
    part = pieces[0].shape[-1]
    groups = len(outputs)
    chunk = min(256, length)

    def body(devs_ref, g_ref, e2_ref, n1_ref, i1_ref, vec_ref, *refs):
        o_refs, piece_refs = refs[:groups], refs[groups : groups + len(pieces)]
        err_ref, errt_ref, sums_ref, *dctx_refs, w, sems = refs[groups + len(pieces) :]
        c = pl.program_id(0)

        @pl.when(c == 0)
        def _():
            copies = blocks.loads(devs_ref, piece_refs, w, sems)
            for copy in copies:
                copy.start()
            for copy in copies:
                copy.wait()

        back = sum(nt(g_ref[:, t * part : (t + 1) * part], w[t]) for t in range(tensor))
        err_in = e2_ref[...] + back
        normed = n1_ref[...]
        err = norm_backward(err_in * vec_ref[1:2, :], normed, i1_ref[...])
        err_ref[...] = err
        err_t = err.T.astype(BF)
        errt_ref[...] = err_t
        for o, d in zip(o_refs, dctx_refs):
            d[...] = nn(o[...], err_t).astype(BF)
        rows = [jnp.sum(a, axis=0, keepdims=True) for a in (err, err_in * normed, err_in)]
        sums = jnp.concatenate(rows + [jnp.zeros((5, width), F32)], axis=0)

        @pl.when(c == 0)
        def _():
            sums_ref[...] = sums

        @pl.when(c > 0)
        def _():
            sums_ref[...] += sums

    rows = lambda n: pl.BlockSpec((chunk, n), lambda c, *_: (c, 0))
    cols = lambda n: pl.BlockSpec((n, chunk), lambda c, *_: (0, c))
    return call(
        body, (length // chunk,), [devs],
        [(grad_pre, rows(grad_pre.shape[1])), (err_two, rows(width)), (normed_one, rows(width)), (inverse_one, rows(1)), (vec, full(vec.shape))]
        + [(o, full(o.shape)) for o in outputs] + [(p, ANY) for p in pieces],
        [((length, width), F32, rows(width)), ((width, length), BF, cols(width)), ((8, width), F32, full((8, width)))]
        + [((o.shape[0], length), BF, cols(o.shape[0])) for o in outputs],
        [pltpu.VMEM((tensor, width, part), BF), pltpu.SemaphoreType.DMA((blocks.n,))],
        (2 * length * width * (grad_pre.shape[1] + width), 2 * grad_pre.size + 18 * length * width), "hidden_gradient",
    )


def local(
    tokens, query_weight, key_weight, value_weight, output_weight, query_bias, value_bias,
    output_bias, first_gain, first_shift, up_weight, up_bias, down_weight, down_bias,
    second_gain, second_shift, cotangent,
):
    dp, tensor = lax.axis_size("dp"), lax.axis_size("tensor")
    count = dp * tensor
    rows = query_weight.shape[0]
    width = rows * dp
    groups = query_weight.shape[1] // HD
    heads = groups * tensor
    slot = output_bias.shape[0]
    cols = query_bias.shape[1]
    me = lax.axis_index(AXES)
    place, devs = position_table(me, count), device_table(me, count)
    direct = rows % 16 == 0

    vectors = jnp.stack([output_bias, first_gain, first_shift, down_bias, second_gain, second_shift])
    extra = small_block(vectors, query_bias, value_bias, up_bias)
    output_turned = output_weight.T
    by_group = [
        jnp.concatenate([w[:, c * HD : (c + 1) * HD] for w in (query_weight, key_weight, value_weight, output_turned)], axis=1)
        for c in range(groups)
    ]
    first_set = gather_blocks(jnp.concatenate([by_group[0], extra], axis=0), count)
    second_set = gather_blocks(jnp.concatenate(by_group[1:], axis=1), count)
    up_set = gather_blocks(up_weight, count)
    down_set = gather_blocks(down_weight.T, count)

    extras = jnp.concatenate([p[:, rows:] for p in first_set], axis=0)
    if direct:
        blocks = Blocks(count, rows, tensor)
        block_place, block_devs = place, devs
    else:
        blocks = Blocks(tensor, width, tensor)
        block_place = block_devs = jnp.arange(tensor, dtype=jnp.int32)

        def whole(pieces):
            ordered = jnp.take(jnp.concatenate(pieces, axis=0)[:, :rows], place, axis=0)
            return [ordered.reshape(dp, tensor, rows, -1).transpose(1, 0, 2, 3).reshape(tensor, width, -1)]

        first_set, second_set, up_set, down_set = (whole(s) for s in (first_set, second_set, up_set, down_set))

    def scattered(keep, send, more=None):
        if not direct:
            stacked = jnp.concatenate([keep, send], axis=0).reshape(tensor, dp, rows, -1)
            stacked = jnp.take(stacked.transpose(1, 0, 2, 3).reshape(count, rows, -1), devs, axis=0)
            if more is not None:
                stacked = jnp.concatenate([stacked, more], axis=1)
            keep, send = stacked[: count // 2], stacked[count // 2 :]
        elif more is not None:
            keep = lax.dynamic_update_slice(keep, more[: count // 2], (0, rows, 0))
            send = lax.dynamic_update_slice(send, more[count // 2 :], (0, rows, 0))
        return scatter_blocks(keep, send, count)

    weights = [(first_set, 0)] + [(second_set, c * PACK) for c in range(groups - 1)]
    vec, bias_rows, up_rows = unpack_small(extras, devs.reshape(count, 1), slot, cols, width, tensor)
    bias_heads = bias_rows[:2].reshape(2, tensor, groups, HD).transpose(2, 1, 0, 3)
    bias_pack = jnp.concatenate(
        [bias_heads[:, :, 0], jnp.zeros_like(bias_heads[:, :, 0]), bias_heads[:, :, 1], jnp.zeros_like(bias_heads[:, :, 0])], axis=-1
    )
    forward = [attention_forward(tokens, p, lane, bias_pack[c], block_devs, blocks) for c, (p, lane) in enumerate(weights)]
    outputs = [f[5] for f in forward]
    normed_one, inverse_one, hidden, hidden_t, act, slope = output_and_up(
        tokens, [f[2] for f in forward], outputs, vec, up_rows, up_set, block_devs, blocks
    )
    layer_out, err_two, err_two_low, err_two_t, sums_two = down_and_norm(act, normed_one, cotangent, vec, down_set, block_devs, blocks)
    grad_down = scattered(*weight_gradient(err_two_t, act, block_place, blocks))
    grad_pre, up_sums = pre_gradient(err_two_low, slope, down_set, block_devs, blocks)
    grad_up = scattered(*weight_gradient(hidden_t, grad_pre, block_place, blocks))
    err_one, err_one_t, sums_one, *context_grads = hidden_gradient(
        grad_pre, err_two, normed_one, inverse_one, vec, outputs, up_set, block_devs, blocks
    )
    tokens_t = tokens.T
    backward = [None] * groups
    for c in reversed(range(groups)):
        qkv, e, ctx, ctxt, inv, _ = forward[c]
        backward[c] = attention_backward(
            tokens_t, err_one_t, qkv, e, inv, ctx, ctxt, context_grads[c], block_place, blocks, EXTRA if direct and c == 0 else 0
        )
    packed = [None] * groups
    for c in reversed(range(1, groups)):
        packed[c] = scattered(*backward[c][:2])
    sums = jnp.stack([b[3][:, 0] for b in backward]).reshape(groups, tensor, 4, HD).transpose(2, 1, 0, 3).reshape(4, width)
    bias_grads = jnp.concatenate([sums[0:1], sums[2:3], jnp.zeros((6, width), F32)], axis=0)
    vec_grads = jnp.concatenate([sums_one[:3], sums_two[:3], jnp.zeros((2, width), F32)], axis=0)
    small = pack_small_grads(vec_grads, bias_grads, up_sums, devs.reshape(count, 1), slot, cols, tensor)
    first = scattered(*backward[0][:2], small)
    grad_tokens = tokens_backward(err_one, [b[2] for b in backward], weights, block_devs, blocks)

    packed[0] = first[:rows]
    tail = first[rows:]
    out = jnp.stack(packed, axis=1).reshape(rows, groups, 4, HD)
    out_query, out_key, out_value, out_output = (out[:, :, i].reshape(rows, groups * HD) for i in range(4))
    vecs = [tail[v // 2, (v % 2) * LANES : (v % 2) * LANES + slot] for v in range(6)]
    return (
        layer_out,
        grad_tokens,
        out_query,
        out_key,
        out_value,
        out_output.T,
        tail[9 : 9 + groups, 32 : 32 + cols],
        tail[9 : 9 + groups, LANES + 32 : LANES + 32 + cols],
        vecs[0],
        vecs[1],
        vecs[2],
        grad_up,
        tail[: up_bias.shape[0], 64 : 64 + cols],
        grad_down.T,
        vecs[3],
        vecs[4],
        vecs[5],
    )


def solution(mesh):
    both, cross, turned, vector = P(AXES, None), P("dp", "tensor"), P("tensor", "dp"), P(AXES)
    return jax.shard_map(
        local,
        mesh=mesh,
        in_specs=(
            both, cross, cross, cross, turned, turned, turned, vector, vector, vector,
            cross, turned, turned, vector, vector, vector, both,
        ),
        out_specs=(
            both, both, cross, cross, cross, turned, turned, turned, vector, vector, vector,
            cross, turned, turned, vector, vector, vector,
        ),
        check_vma=False,
    )
```

time: 755 us -> 435 us (0.58); the launches traced: 741 us -> 430 us
  matrix products: 259 us -> 0 us
  Pallas kernels: 0 us -> 220 us
  local copies, waits for them, and re-layouts: 235 us -> 35.6 us
  other arithmetic: 132 us -> 34.4 us
  starting transfers between devices: 43 us -> 60.1 us
  waiting for transfers between devices: 69 us -> 78.1 us
    dot_general x79 -> x0, matrix products: 236 us -> none  [the longest x21 67.4 us: contract_cols(): lax.dot_general(left, right, (((1,), (1,)), ((), ())), preferred_element_...]
    pallas_call x0 -> x15, Pallas kernels: none -> 220 us  [call(): pl.pallas_call(body, grid_spec=pltpu.PrefetchScalarGridSpec(num_scalar_pr...]
    convert_element_type x21 -> x20, other arithmetic: 70.4 us -> 15.1 us  [scatter_blocks(): send = sum((t[half:2 * half].astype(F32) for t in terms)).astype(BF)]
    concatenate x35 -> x2, local copies, waits for them, and re-layouts: 46.2 us -> 0.15 us  [the longest x1 0.08 us: local(): jnp.concatenate([sums[0:1], sums[2:3], jnp.zeros((6, width), F32)], axis=0)]
    scatter x5 -> x0, local copies, waits for them, and re-layouts: 37.1 us -> none  [the longest x4 36.1 us: blocks_of(): return jnp.zeros_like(stacked).at[place].set(stacked)]
    slice x52 -> x19, local copies, waits for them, and re-layouts: 45.2 us -> 11 us  [the longest x4 2.55 us: local(): extras = jnp.concatenate([p[:, rows:] for p in first_set], axis=0)]
    sub x1 -> x0, matrix products: 23.8 us -> none  [local(): probs = jax.nn.softmax(scores, axis=-1).astype(BF)]
    unnamed x294 -> x63, local copies, waits for them, and re-layouts: 36 us -> 14.4 us
  transfers between devices with their start and end apart: 40 -> 49, of which waited for: 15 -> 18; matrix products, arithmetic and copies ran while one was open for 48% -> 14% of each run, Pallas kernels for 0% -> 45%
where the time goes in v2:
time: 435 us; the launch traced here: 430 us
  Pallas kernels  220 us (51%)
  waiting for transfers between devices  78.1 us (18%)
  starting transfers between devices  60.1 us (14%)
  local copies, waits for them, and re-layouts  35.6 us (8%)
  other arithmetic  34.4 us (8%)
    pallas_call x15, Pallas kernels, call(): pl.pallas_call(body, grid_spec=pltpu.PrefetchScalarGridSpec(num_scalar_pr...  220 us
    ppermute x49, waiting for transfers between devices, exchange(): lax.ppermute(array, AXES, [(d, partner(d, stage)) for d in range(count)])  78.1 us
    ppermute x49, starting transfers between devices, exchange(): lax.ppermute(array, AXES, [(d, partner(d, stage)) for d in range(count)])  60.1 us
    convert_element_type x20, other arithmetic, scatter_blocks(): send = sum((t[half:2 * half].astype(F32) for t in terms)).astype(BF)  15.1 us
    unnamed x63, local copies, waits for them, and re-layouts  14.4 us
  transfers between devices with their start and end apart: 49, of which 18 were waited for; matrix products, arithmetic and copies ran while one was open for 14% of the time, Pallas kernels for 45%

profile of v2, /device:TPU:0, one launch (start us, length us, event | category | flops | bytes accessed | tf_op | source)
XLA Modules:
  0.0 429.7 jit_solution(15164709276255916355)
XLA Ops:
  5.9 4.1 collective-permute-start
  13.2 9.3 %collective-permute-start.1 = (bf16[2,112,256]{2,1,0:T(8,128)(2,1)S(1)}, bf16[2,112,256]{2,1,0:T(8,128)(2,1)S(1)}, u32[]{:S(2)}, u32[]{:S(2)}) collective-permute-start(bf16[2,112,256]{2,1,0:T(8,128)(2,1)S(1)} %pad_maximum_fusion.13), channel_id=1, source_target_pairs={{0,8},{1,9},{2,10},{3,11},{4,12},{5,13},{6,14},{7,15},{8,0},{9,1},... | collective-permute-start | bytes 344072 | tf_op jit(solution)/shard_map/ppermute | solution.py:68
  22.5 3.6 collective-permute-done.12
  34.6 4.6 %collective-permute-done.13 = bf16[2,96,768]{2,1,0:T(8,128)(2,1)S(1)} collective-permute-done((bf16[2,96,768]{2,1,0:T(8,128)(2,1)S(1)}, bf16[2,96,768]{2,1,0:T(8,128)(2,1)S(1)}, u32[]{:S(2)}, u32[]{:S(2)}) %collective-permute-start.13) | collective-permute-done | bytes 294944 | tf_op jit(solution)/shard_map/ppermute | solution.py:68
  52.1 7.3 %collective-permute-done.8 = bf16[4,96,512]{2,1,0:T(8,128)(2,1)} collective-permute-done((bf16[4,96,512]{2,1,0:T(8,128)(2,1)S(1)}, bf16[4,96,512]{2,1,0:T(8,128)(2,1)}, u32[]{:S(2)}, u32[]{:S(2)}) %collective-permute-start.8) | collective-permute-done | bytes 393248 | tf_op jit(solution)/shard_map/ppermute | solution.py:68
  77.4 3.5 unpack_small.1
  86.9 16.6 %attention_forward.3 = (bf16[4,1024,256]{2,1,0:T(8,128)(2,1)}, bf16[4,1024,1024]{2,1,0:T(8,128)(2,1)}, bf16[1024,256]{1,0:T(8,128)(2,1)}, f32[256,1024]{1,0:T(8,...) custom-call(s32[32]{0:T(128)} %or_xor_fusion.1.devs_ref, bf16[1024,768]{1,0:T(8,128)(2,1)} %x_ref.7, ...), custom_call_target="tpu_custom_call" | custom-call | flops 5905580032 | bytes 8388608 | tf_op jit(solution)/shard_map/attention_forward/pallas_call | solution.py:39
  105.1 16.7 %attention_forward.5 = (bf16[4,1024,256]{2,1,0:T(8,128)(2,1)}, bf16[4,1024,1024]{2,1,0:T(8,128)(2,1)}, bf16[1024,256]{1,0:T(8,128)(2,1)}, f32[256,1024]{1,0:T(8,...) custom-call(s32[32]{0:T(128)} %or_xor_fusion.1.devs_ref, bf16[1024,768]{1,0:T(8,128)(2,1)} %x_ref.7, ...), custom_call_target="tpu_custom_call" | custom-call | flops 5905580032 | bytes 8388608 | tf_op jit(solution)/shard_map/attention_forward/pallas_call | solution.py:39
  121.8 16.6 %attention_forward.4 = (bf16[4,1024,256]{2,1,0:T(8,128)(2,1)}, bf16[4,1024,1024]{2,1,0:T(8,128)(2,1)}, bf16[1024,256]{1,0:T(8,128)(2,1)}, f32[256,1024]{1,0:T(8,...) custom-call(s32[32]{0:T(128)} %or_xor_fusion.1.devs_ref, bf16[1024,768]{1,0:T(8,128)(2,1)} %x_ref.7, ...), custom_call_target="tpu_custom_call" | custom-call | flops 5905580032 | bytes 8388608 | tf_op jit(solution)/shard_map/attention_forward/pallas_call | solution.py:39
  139.4 18.1 %output_and_up.1 = (f32[1024,768]{1,0:T(8,128)}, f32[1024,1]{1,0:T(8,128)}, bf16[1024,768]{1,0:T(8,128)(2,1)}, bf16[768,1024]{1,0:T(8,128)(2,1)}, bf16[1024,3072...) custom-call(s32[32]{0:T(128)} %or_xor_fusion.1.devs_ref, bf16[1024,768]{1,0:T(8,128)(2,1)} %x_ref.7, ...), custom_call_target="tpu_custom_call" | custom-call | flops 6039797760 | bytes 25165824 | tf_op jit(solution)/shard_map/output_and_up/pallas_call | solution.py:39
  159.0 15.6 %down_and_norm.1 = (bf16[1024,768]{1,0:T(8,128)(2,1)}, f32[1024,768]{1,0:T(8,128)}, bf16[1024,768]{1,0:T(8,128)(2,1)}, bf16[768,1024]{1,0:T(8,128)(2,1)}, f32[8,768]{1,0:T(8,128)}) custom-call(s32[32]{0:T(128)} %or_xor_fusion.1.devs_ref, bf16[1024,3072]{1,0:T(8,128)(2,1)} %get-tuple-element.81.act_ref.r_ref, f32[1024,768]{1,0:T(8,128)} %get-tuple-element.82.n1_ref, ...), custom_call_target="tpu_custom_call" | custom-call | flops 4831838208 | bytes 18874368 | tf_op jit(solution)/shard_map/down_and_norm/pallas_call | solution.py:39
  174.7 9.9 %weight_gradient.3 = (bf16[16,96,768]{2,1,0:T(8,128)(2,1)}, bf16[16,96,768]{2,1,0:T(8,128)(2,1)}) custom-call(s32[32]{0:T(128)} %shift-left_or_fusion.place_ref, bf16[768,1024]{1,0:T(8,128)(2,1)} %get-tuple-element.124.l_ref, bf16[1024,3072]{1,0:T(8,128)(2,1)} %get-tuple-element.81.act_ref.r_ref), custom_call_target="tpu_custom_call" | custom-call | flops 4831838208 | bytes 12582912 | tf_op jit(solution)/shard_map/weight_gradient/pallas_call | solution.py:39
  184.7 12.9 %pre_gradient.1 = (bf16[1024,3072]{1,0:T(8,128)(2,1)}, f32[8,768]{1,0:T(8,128)}) custom-call(s32[32]{0:T(128)} %or_xor_fusion.1.devs_ref, bf16[1024,768]{1,0:T(8,128)(2,1)} %get-tuple-element.84.e_ref, bf16[1024,3072]{1,0:T(8,128)(2,1)} %get-tuple-element.85.s_ref, bf16[8,96,768]{2,1,0:T(8,128)(2,1)} %pad_maximum_fusion.1.refs_0_, ...), custom_call_target="tpu_custom_call" | custom-call | flops 4831838208 | bytes 17301504 | tf_op jit(solution)/shard_map/pre_gradient/pallas_call | solution.py:39
  197.6 9.9 %weight_gradient.2 = (bf16[16,96,768]{2,1,0:T(8,128)(2,1)}, bf16[16,96,768]{2,1,0:T(8,128)(2,1)}) custom-call(s32[32]{0:T(128)} %shift-left_or_fusion.place_ref, bf16[768,1024]{1,0:T(8,128)(2,1)} %get-tuple-element.121.l_ref, bf16[1024,3072]{1,0:T(8,128)(2,1)} %get-tuple-element.86.g_ref.r_ref), custom_call_target="tpu_custom_call" | custom-call | flops 4831838208 | bytes 12582912 | tf_op jit(solution)/shard_map/weight_gradient/pallas_call | solution.py:39
  208.0 18.2 %hidden_gradient.1 = (f32[1024,768]{1,0:T(8,128)}, bf16[768,1024]{1,0:T(8,128)(2,1)}, f32[8,768]{1,0:T(8,128)}, bf16[256,1024]{1,0:T(8,128)(2,1)}, bf16[256,1024]{1,0:T(8,128)(2,1)}, /*index=5*/bf16[256,1024]{1,0:T(8,128)(2,1)}) custom-call(s32[32]{0:T(128)} %or_xor_fusion.1.devs_ref, bf16[1024,3072]{1,0:T(8,128)(2,1)} %get-tuple-element.86.g_ref.r_ref, ...), custom_call_target="tpu_custom_call" | custom-call | flops 6039797760 | bytes 20447232 | tf_op jit(solution)/shard_map/hidden_gradient/pallas_call | solution.py:39
  226.2 22.1 %attention_backward.5 = (bf16[16,96,256]{2,1,0:T(8,128)(2,1)}, bf16[16,96,256]{2,1,0:T(8,128)(2,1)}, bf16[4,1024,256]{2,1,0:T(8,128)(2,1)}, f32[4,8,256]{2,1,0:T(8,128)}) custom-call(s32[32]{0:T(128)} %shift-left_or_fusion.place_ref, bf16[768,1024]{1,0:T(8,128)(2,1)} %bitcast.62, bf16[768,1024]{1,0:T(8,128)(2,1)} %get-tuple-element.90.et_ref, ...), custom_call_target="tpu_custom_call" | custom-call | flops 10200547328 | bytes 8388608 | tf_op jit(solution)/shard_map/attention_backward/pallas_call | solution.py:39
  249.2 21.8 %attention_backward.4 = (bf16[16,96,256]{2,1,0:T(8,128)(2,1)}, bf16[16,96,256]{2,1,0:T(8,128)(2,1)}, bf16[4,1024,256]{2,1,0:T(8,128)(2,1)}, f32[4,8,256]{2,1,0:T(8,128)}) custom-call(s32[32]{0:T(128)} %shift-left_or_fusion.place_ref, bf16[768,1024]{1,0:T(8,128)(2,1)} %bitcast.63, bf16[768,1024]{1,0:T(8,128)(2,1)} %get-tuple-element.90.et_ref, ...), custom_call_target="tpu_custom_call" | custom-call | flops 10200547328 | bytes 8388608 | tf_op jit(solution)/shard_map/attention_backward/pallas_call | solution.py:39
  271.9 22.2 %attention_backward.3 = (bf16[16,112,256]{2,1,0:T(8,128)(2,1)}, bf16[16,112,256]{2,1,0:T(8,128)(2,1)}, bf16[4,1024,256]{2,1,0:T(8,128)(2,1)}, f32[4,8,256]{2,1,0:T(8,128)}) custom-call(s32[32]{0:T(128)} %shift-left_or_fusion.place_ref, bf16[768,1024]{1,0:T(8,128)(2,1)} %bitcast.64, bf16[768,1024]{1,0:T(8,128)(2,1)} %get-tuple-element.90.et_ref, ...), custom_call_target="tpu_custom_call" | custom-call | flops 10200547328 | bytes 8388608 | tf_op jit(solution)/shard_map/attention_backward/pallas_call | solution.py:39
  302.0 12.8 %tokens_backward.1 = f32[1024,768]{1,0:T(8,128)} custom-call(s32[32]{0:T(128)} %or_xor_fusion.1.devs_ref, f32[1024,768]{1,0:T(8,128)} %get-tuple-element.89.err_ref, bf16[4,1024,256]{2,1,0:T(8,128)(2,1)} %get-tuple-element.96.refs_0_, bf16[4,1024,256]{2,1,0:T(8,128)(2,1)} %get-tuple-element.102.refs_1_, bf16[4,1024,256]{2,1,0:T(8,128)(2,1)} %get-tuple-element.108.refs_2_, ...), custom_call_target="tpu_custom_call" | custom-call | flops 4831838208 | bytes 11010048 | tf_op jit(solution)/shard_map/tokens_backward/pallas_call | solution.py:39
  319.0 3.7 collective-permute-done.30
  324.4 4.4 %collective-permute-done.35 = bf16[8,96,256]{2,1,0:T(8,128)(2,1)S(1)} collective-permute-done((bf16[8,96,256]{2,1,0:T(8,128)(2,1)S(1)}, bf16[8,96,256]{2,1,0:T(8,128)(2,1)S(1)}, u32[]{:S(2)}, u32[]{:S(2)}) %collective-permute-start.35) | collective-permute-done | bytes 393248 | tf_op jit(solution)/shard_map/ppermute | solution.py:68
  330.5 5.6 %collective-permute-done.25 = bf16[8,112,256]{2,1,0:T(8,128)(2,1)S(1)} collective-permute-done((bf16[8,112,256]{2,1,0:T(8,128)(2,1)S(1)}, bf16[8,112,256]{2,1,0:T(8,128)(2,1)S(1)}, u32[]{:S(2)}, u32[]{:S(2)}) %collective-permute-start.25) | collective-permute-done | bytes 458784 | tf_op jit(solution)/shard_map/ppermute | solution.py:68
  372.1 20.6 %collective-permute-done.40 = bf16[8,96,768]{2,1,0:T(8,128)(2,1)} collective-permute-done((bf16[8,96,768]{2,1,0:T(8,128)(2,1)}, bf16[8,96,768]{2,1,0:T(8,128)(2,1)}, u32[]{:S(2)}, u32[]{:S(2)}) %collective-permute-start.40) | collective-permute-done | bytes 1179680 | tf_op jit(solution)/shard_map/ppermute | solution.py:68
  398.8 5.5 %collective-permute-done.41 = bf16[4,96,768]{2,1,0:T(8,128)(2,1)S(1)} collective-permute-done((bf16[4,96,768]{2,1,0:T(8,128)(2,1)S(1)}, bf16[4,96,768]{2,1,0:T(8,128)(2,1)S(1)}, u32[]{:S(2)}, u32[]{:S(2)}) %collective-permute-start.41) | collective-permute-done | bytes 589856 | tf_op jit(solution)/shard_map/ppermute | solution.py:68
  (246 shorter events, 142.5 us)
Async XLA Ops:
  10.2 18.0 %collective-permute-start.6 = (bf16[1,96,512]{2,1,0:T(8,128)(2,1)S(1)}, bf16[1,96,512]{2,1,0:T(8,128)(2,1)S(1)}, u32[]{:S(2)}, u32[]{:S(2)}) collective-permute-start(bf16[1,96,512]{2,1,0:T(8,128)(2,1)S(1)} %bitcast.65), channel_id=1, source_target_pairs={{0,16},{1,17},{2,18},{3,19},{4,20},{5,21},{6,22},{7,23},{8,24},{9,... | collective-permute-start | bytes 294920 | tf_op jit(solution)/shard_map/ppermute | solution.py:68
  13.2 19.7 %collective-permute-start.1 = (bf16[2,112,256]{2,1,0:T(8,128)(2,1)S(1)}, bf16[2,112,256]{2,1,0:T(8,128)(2,1)S(1)}, u32[]{:S(2)}, u32[]{:S(2)}) collective-permute-start(bf16[2,112,256]{2,1,0:T(8,128)(2,1)S(1)} %pad_maximum_fusion.13), channel_id=1, source_target_pairs={{0,8},{1,9},{2,10},{3,11},{4,12},{5,13},{6,14},{7,15},{8,0},{9,1},... | collective-permute-start | bytes 344072 | tf_op jit(solution)/shard_map/ppermute | solution.py:68
  30.5 19.2 %collective-permute-start.19 = (bf16[2,96,768]{2,1,0:T(8,128)(2,1)S(1)}, bf16[2,96,768]{2,1,0:T(8,128)(2,1)S(1)}, u32[]{:S(2)}, u32[]{:S(2)}) collective-permute-start(bf16[2,96,768]{2,1,0:T(8,128)(2,1)S(1)} %pad_maximum_fusion.9), channel_id=1, source_target_pairs={{0,8},{1,9},{2,10},{3,11},{4,12},{5,13},{6,14},{7,15},{8,0},{9,1},... | collective-permute-start | bytes 884744 | tf_op jit(solution)/shard_map/ppermute | solution.py:68
  40.1 22.1 %collective-permute-start.14 = (bf16[4,96,768]{2,1,0:T(8,128)(2,1)}, bf16[4,96,768]{2,1,0:T(8,128)(2,1)}, u32[]{:S(2)}, u32[]{:S(2)}) collective-permute-start(bf16[4,96,768]{2,1,0:T(8,128)(2,1)} %pad_maximum_fusion.3), channel_id=1, source_target_pairs={{0,4},{1,3},{2,6},{3,1},{4,0},{5,7},{6,2},{7,5},{8,12},{9,11},{10,... | collective-permute-start | bytes 1769480 | tf_op jit(solution)/shard_map/ppermute | solution.py:68
  46.8 23.8 %collective-permute-start.4 = (bf16[8,112,256]{2,1,0:T(8,128)(2,1)S(1)}, bf16[8,112,256]{2,1,0:T(8,128)(2,1)}, u32[]{:S(2)}, u32[]{:S(2)}) collective-permute-start(bf16[8,112,256]{2,1,0:T(8,128)(2,1)S(1)} %pad_maximum_fusion.5.refs_0_.refs_3_), channel_id=1, source_target_pairs={{0,1},{1,0},{2,3},{3,2},{4,5},{5,4},{6,7},{7,6},{8,9},{9,8},{10,11... | collective-permute-start | bytes 1376264 | tf_op jit(solution)/shard_map/ppermute | solution.py:68
  50.6 22.3 %collective-permute-start.20 = (bf16[4,96,768]{2,1,0:T(8,128)(2,1)}, bf16[4,96,768]{2,1,0:T(8,128)(2,1)}, u32[]{:S(2)}, u32[]{:S(2)}) collective-permute-start(bf16[4,96,768]{2,1,0:T(8,128)(2,1)} %pad_maximum_fusion.4), channel_id=1, source_target_pairs={{0,4},{1,3},{2,6},{3,1},{4,0},{5,7},{6,2},{7,5},{8,12},{9,11},{10,... | collective-permute-start | bytes 1769480 | tf_op jit(solution)/shard_map/ppermute | solution.py:68
  60.5 21.2 %collective-permute-start.9 = (bf16[8,96,512]{2,1,0:T(8,128)(2,1)S(1)}, bf16[8,96,512]{2,1,0:T(8,128)(2,1)S(1)}, u32[]{:S(2)}, u32[]{:S(2)}) collective-permute-start(bf16[8,96,512]{2,1,0:T(8,128)(2,1)S(1)} %pad_maximum_fusion.2.refs_0_.refs_7_.refs_11_), channel_id=1, source_target_pairs={{0,2},{1,5},{2,0},{3,7},{4,6},{5,1},{6,4},{7,3},{8,10},{9,13},{10,... | collective-permute-start | bytes 2359304 | tf_op jit(solution)/shard_map/ppermute | solution.py:68
  64.4 21.4 %collective-permute-start.15 = (bf16[8,96,768]{2,1,0:T(8,128)(2,1)}, bf16[8,96,768]{2,1,0:T(8,128)(2,1)}, u32[]{:S(2)}, u32[]{:S(2)}) collective-permute-start(bf16[8,96,768]{2,1,0:T(8,128)(2,1)} %pad_maximum_fusion.refs_6_.refs_3_), channel_id=1, source_target_pairs={{0,2},{1,5},{2,0},{3,7},{4,6},{5,1},{6,4},{7,3},{8,10},{9,13},{10,... | collective-permute-start | bytes 3538952 | tf_op jit(solution)/shard_map/ppermute | solution.py:68
  70.6 33.0 %collective-permute-start.10 = (bf16[8,96,512]{2,1,0:T(8,128)(2,1)S(1)}, bf16[8,96,512]{2,1,0:T(8,128)(2,1)S(1)}, u32[]{:S(2)}, u32[]{:S(2)}) collective-permute-start(bf16[8,96,512]{2,1,0:T(8,128)(2,1)S(1)} %pad_maximum_fusion.2.refs_0_.refs_7_.refs_11_), channel_id=1, source_target_pairs={{0,1},{1,0},{2,3},{3,2},{4,5},{5,4},{6,7},{7,6},{8,9},{9,8},{10,11... | collective-permute-start | bytes 2359304 | tf_op jit(solution)/shard_map/ppermute | solution.py:68
  72.8 65.6 %collective-permute-start.16 = (bf16[8,96,768]{2,1,0:T(8,128)(2,1)}, bf16[8,96,768]{2,1,0:T(8,128)(2,1)}, u32[]{:S(2)}, u32[]{:S(2)}) collective-permute-start(bf16[8,96,768]{2,1,0:T(8,128)(2,1)} %pad_maximum_fusion.refs_6_.refs_3_), channel_id=1, source_target_pairs={{0,1},{1,0},{2,3},{3,2},{4,5},{5,4},{6,7},{7,6},{8,9},{9,8},{10,11... | collective-permute-start | bytes 3538952 | tf_op jit(solution)/shard_map/ppermute | solution.py:68
  75.1 28.6 %collective-permute-start.21 = (bf16[8,96,768]{2,1,0:T(8,128)(2,1)}, bf16[8,96,768]{2,1,0:T(8,128)(2,1)}, u32[]{:S(2)}, u32[]{:S(2)}) collective-permute-start(bf16[8,96,768]{2,1,0:T(8,128)(2,1)} %pad_maximum_fusion.1.refs_0_), channel_id=1, source_target_pairs={{0,2},{1,5},{2,0},{3,7},{4,6},{5,1},{6,4},{7,3},{8,10},{9,13},{10,... | collective-permute-start | bytes 3538952 | tf_op jit(solution)/shard_map/ppermute | solution.py:68
  81.8 22.4 %collective-permute-start.11 = (bf16[8,96,512]{2,1,0:T(8,128)(2,1)S(1)}, bf16[8,96,512]{2,1,0:T(8,128)(2,1)S(1)}, u32[]{:S(2)}, u32[]{:S(2)}) collective-permute-start(bf16[8,96,512]{2,1,0:T(8,128)(2,1)S(1)} %collective-permute-done.9.refs_1_.refs_8_.refs_12_), channel_id=1, source_target_pairs={{0,1},{1,0},{2,3},{3,2},{4,5},{5,4},{6,7},{7,6},{8,9},{9,8},{10,11... | collective-permute-start | bytes 2359304 | tf_op jit(solution)/shard_map/ppermute | solution.py:68
  85.8 52.6 %collective-permute-start.17 = (bf16[8,96,768]{2,1,0:T(8,128)(2,1)}, bf16[8,96,768]{2,1,0:T(8,128)(2,1)S(1)}, u32[]{:S(2)}, u32[]{:S(2)}) collective-permute-start(bf16[8,96,768]{2,1,0:T(8,128)(2,1)} %collective-permute-done.15.refs_7_.refs_4_), channel_id=1, source_target_pairs={{0,1},{1,0},{2,3},{3,2},{4,5},{5,4},{6,7},{7,6},{8,9},{9,8},{10,11... | collective-permute-start | bytes 3538952 | tf_op jit(solution)/shard_map/ppermute | solution.py:68
  103.6 54.0 %collective-permute-start.22 = (bf16[8,96,768]{2,1,0:T(8,128)(2,1)}, bf16[8,96,768]{2,1,0:T(8,128)(2,1)S(1)}, u32[]{:S(2)}, u32[]{:S(2)}) collective-permute-start(bf16[8,96,768]{2,1,0:T(8,128)(2,1)} %pad_maximum_fusion.1.refs_0_), channel_id=1, source_target_pairs={{0,1},{1,0},{2,3},{3,2},{4,5},{5,4},{6,7},{7,6},{8,9},{9,8},{10,11... | collective-permute-start | bytes 3538952 | tf_op jit(solution)/shard_map/ppermute | solution.py:68
  103.7 53.9 %collective-permute-start.23 = (bf16[8,96,768]{2,1,0:T(8,128)(2,1)}, bf16[8,96,768]{2,1,0:T(8,128)(2,1)S(1)}, u32[]{:S(2)}, u32[]{:S(2)}) collective-permute-start(bf16[8,96,768]{2,1,0:T(8,128)(2,1)} %collective-permute-done.21.refs_1_), channel_id=1, source_target_pairs={{0,1},{1,0},{2,3},{3,2},{4,5},{5,4},{6,7},{7,6},{8,9},{9,8},{10,11... | collective-permute-start | bytes 3538952 | tf_op jit(solution)/shard_map/ppermute | solution.py:68
  184.6 164.8 %collective-permute-start.44 = (bf16[16,96,768]{2,1,0:T(8,128)(2,1)}, bf16[16,96,768]{2,1,0:T(8,128)(2,1)}, u32[]{:S(2)}, u32[]{:S(2)}) collective-permute-start(bf16[16,96,768]{2,1,0:T(8,128)(2,1)} %get-tuple-element.126), channel_id=1, source_target_pairs={{0,1},{1,0},{2,3},{3,2},{4,5},{5,4},{6,7},{7,6},{8,9},{9,8},{10,11... | collective-permute-start | bytes 7077896 | tf_op jit(solution)/shard_map/ppermute | solution.py:68
  207.5 146.1 %collective-permute-start.39 = (bf16[16,96,768]{2,1,0:T(8,128)(2,1)}, bf16[16,96,768]{2,1,0:T(8,128)(2,1)}, u32[]{:S(2)}, u32[]{:S(2)}) collective-permute-start(bf16[16,96,768]{2,1,0:T(8,128)(2,1)} %get-tuple-element.123), channel_id=1, source_target_pairs={{0,1},{1,0},{2,3},{3,2},{4,5},{5,4},{6,7},{7,6},{8,9},{9,8},{10,11... | collective-permute-start | bytes 7077896 | tf_op jit(solution)/shard_map/ppermute | solution.py:68
  295.2 19.5 %collective-permute-start.29 = (bf16[16,96,256]{2,1,0:T(8,128)(2,1)S(1)}, bf16[16,96,256]{2,1,0:T(8,128)(2,1)S(1)}, u32[]{:S(2)}, u32[]{:S(2)}) collective-permute-start(bf16[16,96,256]{2,1,0:T(8,128)(2,1)S(1)} %copy-done.27), channel_id=1, source_target_pairs={{0,1},{1,0},{2,3},{3,2},{4,5},{5,4},{6,7},{7,6},{8,9},{9,8},{10,11... | collective-permute-start | bytes 2359304 | tf_op jit(solution)/shard_map/ppermute | solution.py:68
  295.4 21.2 %collective-permute-start.34 = (bf16[16,96,256]{2,1,0:T(8,128)(2,1)S(1)}, bf16[16,96,256]{2,1,0:T(8,128)(2,1)S(1)}, u32[]{:S(2)}, u32[]{:S(2)}) collective-permute-start(bf16[16,96,256]{2,1,0:T(8,128)(2,1)S(1)} %copy-done.26), channel_id=1, source_target_pairs={{0,1},{1,0},{2,3},{3,2},{4,5},{5,4},{6,7},{7,6},{8,9},{9,8},{10,11... | collective-permute-start | bytes 2359304 | tf_op jit(solution)/shard_map/ppermute | solution.py:68
  317.3 18.8 %collective-permute-start.25 = (bf16[8,112,256]{2,1,0:T(8,128)(2,1)S(1)}, bf16[8,112,256]{2,1,0:T(8,128)(2,1)S(1)}, u32[]{:S(2)}, u32[]{:S(2)}) collective-permute-start(bf16[8,112,256]{2,1,0:T(8,128)(2,1)S(1)} %add_convert_fusion.4), channel_id=1, source_target_pairs={{0,2},{1,5},{2,0},{3,7},{4,6},{5,1},{6,4},{7,3},{8,10},{9,13},{10,... | collective-permute-start | bytes 1376264 | tf_op jit(solution)/shard_map/ppermute | solution.py:68
  351.1 18.7 %collective-permute-start.45 = (bf16[8,96,768]{2,1,0:T(8,128)(2,1)S(1)}, bf16[8,96,768]{2,1,0:T(8,128)(2,1)}, u32[]{:S(2)}, u32[]{:S(2)}) collective-permute-start(bf16[8,96,768]{2,1,0:T(8,128)(2,1)S(1)} %add_convert_fusion), channel_id=1, source_target_pairs={{0,2},{1,5},{2,0},{3,7},{4,6},{5,1},{6,4},{7,3},{8,10},{9,13},{10,... | collective-permute-start | bytes 3538952 | tf_op jit(solution)/shard_map/ppermute | solution.py:68
  356.2 36.5 %collective-permute-start.40 = (bf16[8,96,768]{2,1,0:T(8,128)(2,1)}, bf16[8,96,768]{2,1,0:T(8,128)(2,1)}, u32[]{:S(2)}, u32[]{:S(2)}) collective-permute-start(bf16[8,96,768]{2,1,0:T(8,128)(2,1)} %add_convert_fusion.1), channel_id=1, source_target_pairs={{0,2},{1,5},{2,0},{3,7},{4,6},{5,1},{6,4},{7,3},{8,10},{9,13},{10,... | collective-permute-start | bytes 3538952 | tf_op jit(solution)/shard_map/ppermute | solution.py:68
  371.3 24.0 %collective-permute-start.46 = (bf16[4,96,768]{2,1,0:T(8,128)(2,1)S(1)}, bf16[4,96,768]{2,1,0:T(8,128)(2,1)S(1)}, u32[]{:S(2)}, u32[]{:S(2)}) collective-permute-start(bf16[4,96,768]{2,1,0:T(8,128)(2,1)S(1)} %add_convert_fusion.2), channel_id=1, source_target_pairs={{0,4},{1,3},{2,6},{3,1},{4,0},{5,7},{6,2},{7,5},{8,12},{9,11},{10,... | collective-permute-start | bytes 1769480 | tf_op jit(solution)/shard_map/ppermute | solution.py:68
  397.2 18.4 %collective-permute-start.47 = (bf16[2,96,768]{2,1,0:T(8,128)(2,1)}, bf16[2,96,768]{2,1,0:T(8,128)(2,1)}, u32[]{:S(2)}, u32[]{:S(2)}) collective-permute-start(bf16[2,96,768]{2,1,0:T(8,128)(2,1)} %add_convert_fusion.7), channel_id=1, source_target_pairs={{0,8},{1,9},{2,10},{3,11},{4,12},{5,13},{6,14},{7,15},{8,0},{9,1},... | collective-permute-start | bytes 884744 | tf_op jit(solution)/shard_map/ppermute | solution.py:68
  (53 other events, 714.6 us)
